TPU v7x, 32 devices: a whole 2x2x4 slice. The times are simulated.
32 devices in a mesh: loop: 8 (over z, y), seg: 4 (over x, core).
Axes of the slice: x: 2, y: 2, z: 4, core: 2. Of those that a mesh axis runs over, the one named last changes fastest.
Arguments:
- dosage: bfloat16 [2048, 8192], P('seg', 'loop'), may hold values from -3 to 3
- weight_tiles: bfloat16 [3, 1024, 1024], P(None, None, 'loop'), may hold values from -0.109375 to 0.109375
- first_tile: int32 [1024], P('loop'), may hold values from 0 to 1
- last_tile: int32 [1024], P('loop'), may hold values from 1 to 2
Outputs:
- covariance: float32 [1024, 1024], P('seg', 'loop')
Inputs may be any that keep to these rules, and one draw needn't show every extreme that they name: `first_tile`: a gene's window always covers its home slot 1.
All inputs are finite; a program needn't handle non-finite values.
Results may differ from a plain program's by a relative error of at most 0.0021.
Values may be sent and summed in bfloat16 or wider, within the bound.
No kernel may reach another device: no remote copies, remote signals or barrier semaphores. Data moves between devices by JAX's collectives and lax.ppermute only.
A program may use at most 64 MiB of HBM per device.

v0:
```python
import functools

import jax
import jax.numpy as jnp
import numpy as np
from jax import lax
from jax.experimental import pallas as pl
from jax.experimental.pallas import tpu as pltpu
from jax.sharding import PartitionSpec as P


AXES = ("loop", "seg")


def ring_next(loop_size, place):
    if place % 2 == 0:
        return place + 2 if place + 2 < loop_size else loop_size - 1
    return place - 2 if place >= 3 else 0


def move(value, sizes, target):
    loop_size, seg_size = sizes
    pairs = []
    for place in range(loop_size):
        for part in range(seg_size):
            to = target(place, part)
            if to is not None and 0 <= to[0] < loop_size:
                pairs.append((place * seg_size + part, to[0] * seg_size + to[1]))
    return lax.ppermute(value, AXES, pairs)


def pair_kernel(n_blocks, where_ref, column_ref, *refs):
    blocks, own_ref, away_refs, sums_ref = refs[:n_blocks], refs[n_blocks], refs[n_blocks + 1 : -1], refs[-1]
    genes = column_ref.shape[0]
    column = column_ref[...]
    for k, block in enumerate(blocks):
        product = lax.dot_general(block[...], column, (((1,), (1,)), ((), ())), preferred_element_type=jnp.float32)
        row = pl.multiple_of(where_ref[2 * k + 1] * genes, genes)
        sums_ref[where_ref[2 * k], pl.ds(row, genes), :] = product
    own_ref[...] = sums_ref[0]
    for j, away_ref in enumerate(away_refs):
        away_ref[...] = sums_ref[j + 1].astype(jnp.bfloat16)


def shards(dosage, weight_tiles, first_tile, last_tile):
    loop_size, seg_size = sizes = (lax.axis_size("loop"), lax.axis_size("seg"))
    place, part = lax.axis_index("loop"), lax.axis_index("seg")
    n_slots, block, genes = weight_tiles.shape
    samples = dosage.shape[0]
    odd, side = place % 2, part % 2
    half = block // 2

    def masked_half(slot):
        tile = lax.dynamic_slice(weight_tiles, (slot, side * half, 0), (1, half, genes))[0]
        covered = (slot >= first_tile) & (slot <= last_tile)
        return jnp.where(covered[None, :], tile, jnp.zeros((), tile.dtype))

    far_slot = odd * (n_slots - 1)
    far_half = masked_half(far_slot)
    near_half = masked_half(n_slots - 1 - far_slot)
    outward = lambda step: lambda l, s: (l + step if l % 2 else l - step, s)
    partner = lambda l, s: (l ^ 1, s)
    sibling = lambda l, s: (l, s ^ 1)

    def product(tile):
        return lax.dot_general(tile, dosage, (((0,), (1,)), ((), ())), preferred_element_type=jnp.float32)

    def term(mine, other):
        lower = jnp.where(side == 0, mine, other)
        upper = jnp.where(side == 0, other, mine)
        return product(jnp.concatenate([lower, upper], axis=0))

    far_half = move(far_half, sizes, outward(1))
    near_half = move(near_half, sizes, partner)
    home_term = product(weight_tiles[n_slots // 2])
    far_half, _ = lax.optimization_barrier((far_half, home_term))
    home_term = move(home_term, sizes, partner)
    far_term = term(far_half, move(far_half, sizes, sibling))
    near_half, _ = lax.optimization_barrier((near_half, far_term))
    far_term = move(far_term, sizes, outward(2))
    near_term = term(near_half, move(near_half, sizes, sibling))
    projection = (near_term + home_term + far_term).astype(jnp.bfloat16)

    column = move(projection, sizes, partner)
    ahead = [ring_next(loop_size, l) for l in range(loop_size)]
    behind = [ahead.index(l) for l in range(loop_size)]
    blocks, sources = [projection], [list(range(loop_size))]
    forth = back = projection
    forth_from = back_from = sources[0]
    for _ in range(loop_size // 2 - 1):
        forth = move(forth, sizes, lambda l, s: (ahead[l], s))
        forth_from = [forth_from[behind[l]] for l in range(loop_size)]
        back = move(back, sizes, lambda l, s: (behind[l], s))
        back_from = [back_from[ahead[l]] for l in range(loop_size)]
        blocks += [forth, back]
        sources += [forth_from, back_from]
    opposite = jnp.where(side == 0, forth, back)
    blocks.append(move(opposite, sizes, lambda l, s: (behind[l] if s % 2 else ahead[l], s)))
    sources.append([forth_from[behind[l]] for l in range(loop_size)])

    per_chunk = loop_size // seg_size
    held = np.array(sources).T ^ 1
    parts = np.arange(seg_size)[None, :, None]
    table = np.stack([(held[:, None, :] // per_chunk) ^ parts, np.broadcast_to((held % per_chunk)[:, None, :], (loop_size, seg_size, loop_size))], axis=-1)
    table = jnp.asarray(table.reshape(loop_size * seg_size, -1), jnp.int32)
    where = lax.dynamic_slice(table, (place * seg_size + part, 0), (1, table.shape[1]))[0]
    rows = loop_size * genes // seg_size
    vmem = pl.BlockSpec(memory_space=pltpu.VMEM)
    own, *away = pl.pallas_call(
        functools.partial(pair_kernel, loop_size),
        out_shape=[jax.ShapeDtypeStruct((rows, genes), jnp.float32)] + [jax.ShapeDtypeStruct((rows, genes), jnp.bfloat16)] * (seg_size - 1),
        in_specs=[pl.BlockSpec(memory_space=pltpu.SMEM)] + [vmem] * (loop_size + 1),
        out_specs=[vmem] * seg_size,
        scratch_shapes=[pltpu.VMEM((seg_size, rows, genes), jnp.float32)],
        compiler_params=pltpu.CompilerParams(vmem_limit_bytes=2 * (loop_size + 1) * genes * samples * 2 + 3 * seg_size * rows * genes * 4),
        name="pair_sums",
    )(where, column, *blocks)
    total = own
    for j in range(1, seg_size):
        total = total + move(away[j - 1], sizes, lambda l, s: (l, s ^ j)).astype(jnp.float32)
    return total / (samples * seg_size)


def solution(mesh):
    return jax.shard_map(
        shards,
        mesh=mesh,
        in_specs=(P("seg", "loop"), P(None, None, "loop"), P("loop"), P("loop")),
        out_specs=P("seg", "loop"),
        check_vma=False,
    )
```

profile of v0, /device:TPU:0, one launch (start us, length us, event | category | flops | bytes accessed | tf_op | source)
XLA Modules:
  0.0 58.4 jit_solution(1834151665222736419)
XLA Ops:
  0.0 0.0 copy-start
  0.0 0.0 copy-start.1
  0.0 0.0 copy-start.2
  0.0 0.7 %copy-done.1 = s32[128]{0:T(128)S(1)} copy-done((s32[128]{0:T(128)S(1)}, s32[128]{0:T(128)}, u32[]{:S(2)}) %copy-start.1) | copy-done | bytes 536
  0.7 0.0 copy-done.2
  0.8 1.0 %bitcast_select_fusion.1 = (bf16[512,128]{1,0:T(8,128)(2,1)S(1)}, bf16[512,128]{1,0:T(8,128)(2,1)S(1)}) fusion(bf16[3,1024,128]{2,1,0:T(8,128)(2,1)} %param.6, s32[]{:T(128)S(6)} %select_n.63, s32[]{:T(128)S(6)} %select_n.64, pred[128]{0:T(512)(128)(4,1)S(1)} %get-tuple-element.23, s32[]{:T(128)S(6)} %select_n.66, pred[128]{0:T(512)(128)(4,1)S(1)} %get-tuple-element.24), kind=kLoop, calls=%fused_computation.14 | loop fusion | flops 131072 | bytes 524556 | tf_op jit(solution)/shard_map/jit(_where)/select_n | solution.py:56
  1.8 0.7 %collective-permute-start.1 = (bf16[512,128]{1,0:T(8,128)(2,1)S(1)}, bf16[512,128]{1,0:T(8,128)(2,1)S(1)}, u32[]{:S(2)}, u32[]{:S(2)}) collective-permute-start(bf16[512,128]{1,0:T(8,128)(2,1)S(1)} %get-tuple-element.18), channel_id=1, source_target_pairs={{4,8},{5,9},{6,10},{7,11},{8,4},{9,5},{10,6},{11,7},{12,16},{13,17... | collective-permute-start | bytes 393224 | tf_op jit(solution)/shard_map/ppermute | solution.py:29
  2.5 0.0 copy-done
  2.5 1.4 %fusion.9 = f32[128,512]{1,0:T(8,128)S(1)} fusion(bf16[512,1024]{1,0:T(8,128)(2,1)S(1)} %copy-done, bf16[3,1024,128]{2,1,0:T(8,128)(2,1)} %param.6), kind=kOutput, calls=%fused_computation.10 | convolution fusion | flops 134217728 | bytes 1572864 | tf_op jit(solution)/shard_map/dot_general | solution.py:66
  3.9 0.0 collective-permute-done.1
  3.9 0.6 collective-permute-start.2
  4.5 8.3 %collective-permute-start = (bf16[512,128]{1,0:T(8,128)(2,1)S(1)}, bf16[512,128]{1,0:T(8,128)(2,1)S(1)}, u32[]{:S(2)}, u32[]{:S(2)}) collective-permute-start(bf16[512,128]{1,0:T(8,128)(2,1)S(1)} %get-tuple-element.17), channel_id=1, source_target_pairs={{0,4},{1,5},{2,6},{3,7},{4,0},{5,1},{6,2},{7,3},{8,12},{9,13},{10,... | collective-permute-start | bytes 393224 | tf_op jit(solution)/shard_map/ppermute | solution.py:29
  12.8 0.0 collective-permute-done.2
  12.9 0.5 fusion.2
  13.3 3.6 %collective-permute-done = bf16[512,128]{1,0:T(8,128)(2,1)S(1)} collective-permute-done((bf16[512,128]{1,0:T(8,128)(2,1)S(1)}, bf16[512,128]{1,0:T(8,128)(2,1)S(1)}, u32[]{:S(2)}, u32[]{:S(2)}) %collective-permute-start) | collective-permute-done | bytes 131104 | tf_op jit(solution)/shard_map/ppermute | solution.py:29
  17.0 0.0 collective-permute-start.3
  17.0 1.7 %collective-permute-start.4 = (f32[128,512]{1,0:T(8,128)S(1)}, f32[128,512]{1,0:T(8,128)S(1)}, u32[]{:S(2)}, u32[]{:S(2)}) collective-permute-start(f32[128,512]{1,0:T(8,128)S(1)} %fusion.9), channel_id=1, source_target_pairs={{0,4},{1,5},{2,6},{3,7},{4,0},{5,1},{6,2},{7,3},{8,12},{9,13},{10,... | collective-permute-start | bytes 786440 | tf_op jit(solution)/shard_map/ppermute | solution.py:29
  18.7 1.3 %collective-permute-start.5 = (f32[128,512]{1,0:T(8,128)S(1)}, f32[128,512]{1,0:T(8,128)S(1)}, u32[]{:S(2)}, u32[]{:S(2)}) collective-permute-start(f32[128,512]{1,0:T(8,128)S(1)} %fusion.2), channel_id=1, source_target_pairs={{4,12},{5,13},{6,14},{7,15},{8,0},{9,1},{10,2},{11,3},{12,20},{13,... | collective-permute-start | bytes 786440 | tf_op jit(solution)/shard_map/ppermute | solution.py:29
  20.0 0.0 collective-permute-done.3
  20.1 5.6 %collective-permute-done.4 = f32[128,512]{1,0:T(8,128)S(1)} collective-permute-done((f32[128,512]{1,0:T(8,128)S(1)}, f32[128,512]{1,0:T(8,128)S(1)}, u32[]{:S(2)}, u32[]{:S(2)}) %collective-permute-start.4) | collective-permute-done | bytes 262176 | tf_op jit(solution)/shard_map/ppermute | solution.py:29
  25.7 3.3 %collective-permute-done.5 = f32[128,512]{1,0:T(8,128)S(1)} collective-permute-done((f32[128,512]{1,0:T(8,128)S(1)}, f32[128,512]{1,0:T(8,128)S(1)}, u32[]{:S(2)}, u32[]{:S(2)}) %collective-permute-start.5) | collective-permute-done | bytes 262176 | tf_op jit(solution)/shard_map/ppermute | solution.py:29
  29.1 0.5 fusion.1.refs_0_
  29.6 0.1 collective-permute-start.8
  29.6 2.0 %collective-permute-start.7 = (bf16[128,512]{1,0:T(8,128)(2,1)S(1)}, bf16[128,512]{1,0:T(8,128)(2,1)S(1)}, u32[]{:S(2)}, u32[]{:S(2)}) collective-permute-start(bf16[128,512]{1,0:T(8,128)(2,1)S(1)} %fusion.1.refs_0_), channel_id=1, source_target_pairs={{0,8},{1,9},{2,10},{3,11},{4,0},{5,1},{6,2},{7,3},{8,16},{9,17},{1... | collective-permute-start | bytes 393224 | tf_op jit(solution)/shard_map/ppermute | solution.py:29
  31.6 2.9 %collective-permute-done.8.refs_2_ = bf16[128,512]{1,0:T(8,128)(2,1)S(1)} collective-permute-done((bf16[128,512]{1,0:T(8,128)(2,1)S(1)}, bf16[128,512]{1,0:T(8,128)(2,1)S(1)}, u32[]{:S(2)}, u32[]{:S(2)}) %collective-permute-start.8) | collective-permute-done | bytes 131104 | tf_op jit(solution)/shard_map/ppermute | solution.py:29
  34.6 0.1 collective-permute-start.10
  34.7 0.0 collective-permute-done.7.refs_1_
  34.7 1.9 %collective-permute-start.9 = (bf16[128,512]{1,0:T(8,128)(2,1)S(1)}, bf16[128,512]{1,0:T(8,128)(2,1)S(1)}, u32[]{:S(2)}, u32[]{:S(2)}) collective-permute-start(bf16[128,512]{1,0:T(8,128)(2,1)S(1)} %collective-permute-done.7.refs_1_), channel_id=1, source_target_pairs={{0,8},{1,9},{2,10},{3,11},{4,0},{5,1},{6,2},{7,3},{8,16},{9,17},{1... | collective-permute-start | bytes 393224 | tf_op jit(solution)/shard_map/ppermute | solution.py:29
  36.6 3.3 %collective-permute-done.10.refs_4_ = bf16[128,512]{1,0:T(8,128)(2,1)S(1)} collective-permute-done((bf16[128,512]{1,0:T(8,128)(2,1)S(1)}, bf16[128,512]{1,0:T(8,128)(2,1)S(1)}, u32[]{:S(2)}, u32[]{:S(2)}) %collective-permute-start.10) | collective-permute-done | bytes 131104 | tf_op jit(solution)/shard_map/ppermute | solution.py:29
  39.9 0.0 collective-permute-start.12
  39.9 0.0 collective-permute-done.9.refs_3_
  39.9 2.3 %collective-permute-start.11 = (bf16[128,512]{1,0:T(8,128)(2,1)S(1)}, bf16[128,512]{1,0:T(8,128)(2,1)S(1)}, u32[]{:S(2)}, u32[]{:S(2)}) collective-permute-start(bf16[128,512]{1,0:T(8,128)(2,1)S(1)} %collective-permute-done.9.refs_3_), channel_id=1, source_target_pairs={{0,8},{1,9},{2,10},{3,11},{4,0},{5,1},{6,2},{7,3},{8,16},{9,17},{1... | collective-permute-start | bytes 393224 | tf_op jit(solution)/shard_map/ppermute | solution.py:29
  42.2 0.0 collective-permute-start.6
  42.2 3.8 %collective-permute-done.12.refs_6_ = bf16[128,512]{1,0:T(8,128)(2,1)S(1)} collective-permute-done((bf16[128,512]{1,0:T(8,128)(2,1)S(1)}, bf16[128,512]{1,0:T(8,128)(2,1)S(1)}, u32[]{:S(2)}, u32[]{:S(2)}) %collective-permute-start.12) | collective-permute-done | bytes 131104 | tf_op jit(solution)/shard_map/ppermute | solution.py:29
  46.0 0.0 collective-permute-done.11.refs_5_
  46.0 1.5 %collective-permute-start.13 = (bf16[128,512]{1,0:T(8,128)(2,1)S(1)}, bf16[128,512]{1,0:T(8,128)(2,1)S(1)}, u32[]{:S(2)}, u32[]{:S(2)}) collective-permute-start(bf16[128,512]{1,0:T(8,128)(2,1)S(1)} %broadcast_select_fusion), channel_id=1, source_target_pairs={{0,8},{1,5},{2,10},{3,7},{4,0},{5,13},{6,2},{7,15},{8,16},{9,1},{1... | collective-permute-start | bytes 393224 | tf_op jit(solution)/shard_map/ppermute | solution.py:29
  47.5 0.7 %fusion.12.where_ref = s32[16]{0:T(128)S(1)} fusion(s32[32,16]{1,0:T(8,128)} %constant.46.clone, s32[]{:T(128)S(6)} %select_n.59), kind=kLoop, calls=%fused_computation.24 | loop fusion | bytes 132 | tf_op jit(solution)/shard_map/squeeze | solution.py:106
  48.1 0.0 collective-permute-done.6.column_ref
  48.2 2.9 %collective-permute-done.13.refs_7_ = bf16[128,512]{1,0:T(8,128)(2,1)S(1)} collective-permute-done((bf16[128,512]{1,0:T(8,128)(2,1)S(1)}, bf16[128,512]{1,0:T(8,128)(2,1)S(1)}, u32[]{:S(2)}, u32[]{:S(2)}) %collective-permute-start.13) | collective-permute-done | bytes 131104 | tf_op jit(solution)/shard_map/ppermute | solution.py:29
  51.0 1.0 %pair_sums.1 = (f32[256,128]{1,0:T(8,128)S(1)}, bf16[256,128]{1,0:T(8,128)(2,1)S(1)}, bf16[256,128]{1,0:T(8,128)(2,1)S(1)}, bf16[256,128]{1,0:T(8,128)(2,1)S(1)}) custom-call(s32[16]{0:T(128)S(1)} %fusion.12.where_ref, bf16[128,512]{1,0:T(8,128)(2,1)S(1)} %collective-permute-done.6.column_ref, bf16[128,512]{1,0:T(8,128)(2,1)S(1)} %fusion.1.refs_0_, ...), custom_call_target="tpu_custom_call" | custom-call | tf_op jit(solution)/shard_map/pair_sums/pallas_call | solution.py:109
  52.0 0.1 collective-permute-start.14
  52.1 1.5 %collective-permute-start.15 = (bf16[256,128]{1,0:T(8,128)(2,1)S(1)}, bf16[256,128]{1,0:T(8,128)(2,1)S(1)}, u32[]{:S(2)}, u32[]{:S(2)}) collective-permute-start(bf16[256,128]{1,0:T(8,128)(2,1)S(1)} %get-tuple-element.15), channel_id=1, source_target_pairs={{0,2},{1,3},{2,0},{3,1},{4,6},{5,7},{6,4},{7,5},{8,10},{9,11},{10,... | collective-permute-start | bytes 196616 | tf_op jit(solution)/shard_map/ppermute | solution.py:29
  53.6 0.3 collective-permute-start.16
  53.9 0.0 collective-permute-done.14
  54.0 2.6 %collective-permute-done.15 = bf16[256,128]{1,0:T(8,128)(2,1)S(1)} collective-permute-done((bf16[256,128]{1,0:T(8,128)(2,1)S(1)}, bf16[256,128]{1,0:T(8,128)(2,1)S(1)}, u32[]{:S(2)}, u32[]{:S(2)}) %collective-permute-start.15) | collective-permute-done | bytes 65568 | tf_op jit(solution)/shard_map/ppermute | solution.py:29
  56.6 1.1 %collective-permute-done.16 = bf16[256,128]{1,0:T(8,128)(2,1)S(1)} collective-permute-done((bf16[256,128]{1,0:T(8,128)(2,1)S(1)}, bf16[256,128]{1,0:T(8,128)(2,1)S(1)}, u32[]{:S(2)}, u32[]{:S(2)}) %collective-permute-start.16) | collective-permute-done | bytes 65568 | tf_op jit(solution)/shard_map/ppermute | solution.py:29
  57.7 0.7 %add_multiply_fusion = f32[256,128]{1,0:T(8,128)} fusion(bf16[256,128]{1,0:T(8,128)(2,1)S(1)} %collective-permute-done.16, bf16[256,128]{1,0:T(8,128)(2,1)S(1)} %collective-permute-done.15, f32[256,128]{1,0:T(8,128)S(1)} %get-tuple-element.13, bf16[256,128]{1,0:T(8,128)(2,1)S(1)} %collective-permute-done.14), kind=kLoop, calls=%fused_computation.15 | loop fusion | flops 229376 | bytes 458752 | tf_op jit(solution)/shard_map/div | solution.py:121
  (4 shorter events, 0.1 us)
Async XLA Ops:
  0.0 2.5 %copy-start = (bf16[512,1024]{1,0:T(8,128)(2,1)S(1)}, bf16[512,1024]{1,0:T(8,128)(2,1)}, u32[]{:S(2)}) copy-start(bf16[512,1024]{1,0:T(8,128)(2,1)} %param.5) | copy-start | bytes 3145732
  0.0 0.7 %copy-start.1 = (s32[128]{0:T(128)S(1)}, s32[128]{0:T(128)}, u32[]{:S(2)}) copy-start(s32[128]{0:T(128)} %param.8) | copy-start | bytes 1540
  0.0 0.8 %copy-start.2 = (s32[128]{0:T(128)S(1)}, s32[128]{0:T(128)}, u32[]{:S(2)}) copy-start(s32[128]{0:T(128)} %param.7) | copy-start | bytes 1540
  1.8 2.1 %collective-permute-start.1 = (bf16[512,128]{1,0:T(8,128)(2,1)S(1)}, bf16[512,128]{1,0:T(8,128)(2,1)S(1)}, u32[]{:S(2)}, u32[]{:S(2)}) collective-permute-start(bf16[512,128]{1,0:T(8,128)(2,1)S(1)} %get-tuple-element.18), channel_id=1, source_target_pairs={{4,8},{5,9},{6,10},{7,11},{8,4},{9,5},{10,6},{11,7},{12,16},{13,17... | collective-permute-start | bytes 393224 | tf_op jit(solution)/shard_map/ppermute | solution.py:29
  3.9 8.9 %collective-permute-start.2 = (bf16[512,128]{1,0:T(8,128)(2,1)S(1)}, bf16[512,128]{1,0:T(8,128)(2,1)S(1)}, u32[]{:S(2)}, u32[]{:S(2)}) collective-permute-start(bf16[512,128]{1,0:T(8,128)(2,1)S(1)} %collective-permute-done.1), channel_id=1, source_target_pairs={{0,1},{1,0},{2,3},{3,2},{4,5},{5,4},{6,7},{7,6},{8,9},{9,8},{10,11... | collective-permute-start | bytes 393224 | tf_op jit(solution)/shard_map/ppermute | solution.py:29
  4.5 12.5 %collective-permute-start = (bf16[512,128]{1,0:T(8,128)(2,1)S(1)}, bf16[512,128]{1,0:T(8,128)(2,1)S(1)}, u32[]{:S(2)}, u32[]{:S(2)}) collective-permute-start(bf16[512,128]{1,0:T(8,128)(2,1)S(1)} %get-tuple-element.17), channel_id=1, source_target_pairs={{0,4},{1,5},{2,6},{3,7},{4,0},{5,1},{6,2},{7,3},{8,12},{9,13},{10,... | collective-permute-start | bytes 393224 | tf_op jit(solution)/shard_map/ppermute | solution.py:29
  17.0 3.0 %collective-permute-start.3 = (bf16[512,128]{1,0:T(8,128)(2,1)S(1)}, bf16[512,128]{1,0:T(8,128)(2,1)S(1)}, u32[]{:S(2)}, u32[]{:S(2)}) collective-permute-start(bf16[512,128]{1,0:T(8,128)(2,1)S(1)} %collective-permute-done), channel_id=1, source_target_pairs={{0,1},{1,0},{2,3},{3,2},{4,5},{5,4},{6,7},{7,6},{8,9},{9,8},{10,11... | collective-permute-start | bytes 393224 | tf_op jit(solution)/shard_map/ppermute | solution.py:29
  17.0 8.7 %collective-permute-start.4 = (f32[128,512]{1,0:T(8,128)S(1)}, f32[128,512]{1,0:T(8,128)S(1)}, u32[]{:S(2)}, u32[]{:S(2)}) collective-permute-start(f32[128,512]{1,0:T(8,128)S(1)} %fusion.9), channel_id=1, source_target_pairs={{0,4},{1,5},{2,6},{3,7},{4,0},{5,1},{6,2},{7,3},{8,12},{9,13},{10,... | collective-permute-start | bytes 786440 | tf_op jit(solution)/shard_map/ppermute | solution.py:29
  18.7 10.3 %collective-permute-start.5 = (f32[128,512]{1,0:T(8,128)S(1)}, f32[128,512]{1,0:T(8,128)S(1)}, u32[]{:S(2)}, u32[]{:S(2)}) collective-permute-start(f32[128,512]{1,0:T(8,128)S(1)} %fusion.2), channel_id=1, source_target_pairs={{4,12},{5,13},{6,14},{7,15},{8,0},{9,1},{10,2},{11,3},{12,20},{13,... | collective-permute-start | bytes 786440 | tf_op jit(solution)/shard_map/ppermute | solution.py:29
  29.6 5.0 %collective-permute-start.8 = (bf16[128,512]{1,0:T(8,128)(2,1)S(1)}, bf16[128,512]{1,0:T(8,128)(2,1)S(1)}, u32[]{:S(2)}, u32[]{:S(2)}) collective-permute-start(bf16[128,512]{1,0:T(8,128)(2,1)S(1)} %fusion.1.refs_0_), channel_id=1, source_target_pairs={{0,4},{1,5},{2,6},{3,7},{4,12},{5,13},{6,14},{7,15},{8,0},{9,1},{1... | collective-permute-start | bytes 393224 | tf_op jit(solution)/shard_map/ppermute | solution.py:29
  29.6 5.0 %collective-permute-start.7 = (bf16[128,512]{1,0:T(8,128)(2,1)S(1)}, bf16[128,512]{1,0:T(8,128)(2,1)S(1)}, u32[]{:S(2)}, u32[]{:S(2)}) collective-permute-start(bf16[128,512]{1,0:T(8,128)(2,1)S(1)} %fusion.1.refs_0_), channel_id=1, source_target_pairs={{0,8},{1,9},{2,10},{3,11},{4,0},{5,1},{6,2},{7,3},{8,16},{9,17},{1... | collective-permute-start | bytes 393224 | tf_op jit(solution)/shard_map/ppermute | solution.py:29
  34.6 5.3 %collective-permute-start.10 = (bf16[128,512]{1,0:T(8,128)(2,1)S(1)}, bf16[128,512]{1,0:T(8,128)(2,1)S(1)}, u32[]{:S(2)}, u32[]{:S(2)}) collective-permute-start(bf16[128,512]{1,0:T(8,128)(2,1)S(1)} %collective-permute-done.8.refs_2_), channel_id=1, source_target_pairs={{0,4},{1,5},{2,6},{3,7},{4,12},{5,13},{6,14},{7,15},{8,0},{9,1},{1... | collective-permute-start | bytes 393224 | tf_op jit(solution)/shard_map/ppermute | solution.py:29
  34.7 5.2 %collective-permute-start.9 = (bf16[128,512]{1,0:T(8,128)(2,1)S(1)}, bf16[128,512]{1,0:T(8,128)(2,1)S(1)}, u32[]{:S(2)}, u32[]{:S(2)}) collective-permute-start(bf16[128,512]{1,0:T(8,128)(2,1)S(1)} %collective-permute-done.7.refs_1_), channel_id=1, source_target_pairs={{0,8},{1,9},{2,10},{3,11},{4,0},{5,1},{6,2},{7,3},{8,16},{9,17},{1... | collective-permute-start | bytes 393224 | tf_op jit(solution)/shard_map/ppermute | solution.py:29
  39.9 6.1 %collective-permute-start.12 = (bf16[128,512]{1,0:T(8,128)(2,1)S(1)}, bf16[128,512]{1,0:T(8,128)(2,1)S(1)}, u32[]{:S(2)}, u32[]{:S(2)}) collective-permute-start(bf16[128,512]{1,0:T(8,128)(2,1)S(1)} %collective-permute-done.10.refs_4_), channel_id=1, source_target_pairs={{0,4},{1,5},{2,6},{3,7},{4,12},{5,13},{6,14},{7,15},{8,0},{9,1},{1... | collective-permute-start | bytes 393224 | tf_op jit(solution)/shard_map/ppermute | solution.py:29
  39.9 6.1 %collective-permute-start.11 = (bf16[128,512]{1,0:T(8,128)(2,1)S(1)}, bf16[128,512]{1,0:T(8,128)(2,1)S(1)}, u32[]{:S(2)}, u32[]{:S(2)}) collective-permute-start(bf16[128,512]{1,0:T(8,128)(2,1)S(1)} %collective-permute-done.9.refs_3_), channel_id=1, source_target_pairs={{0,8},{1,9},{2,10},{3,11},{4,0},{5,1},{6,2},{7,3},{8,16},{9,17},{1... | collective-permute-start | bytes 393224 | tf_op jit(solution)/shard_map/ppermute | solution.py:29
  42.2 6.0 %collective-permute-start.6 = (bf16[128,512]{1,0:T(8,128)(2,1)S(1)}, bf16[128,512]{1,0:T(8,128)(2,1)S(1)}, u32[]{:S(2)}, u32[]{:S(2)}) collective-permute-start(bf16[128,512]{1,0:T(8,128)(2,1)S(1)} %fusion.1.refs_0_), channel_id=1, source_target_pairs={{0,4},{1,5},{2,6},{3,7},{4,0},{5,1},{6,2},{7,3},{8,12},{9,13},{10,... | collective-permute-start | bytes 393224 | tf_op jit(solution)/shard_map/ppermute | solution.py:29
  46.0 5.0 %collective-permute-start.13 = (bf16[128,512]{1,0:T(8,128)(2,1)S(1)}, bf16[128,512]{1,0:T(8,128)(2,1)S(1)}, u32[]{:S(2)}, u32[]{:S(2)}) collective-permute-start(bf16[128,512]{1,0:T(8,128)(2,1)S(1)} %broadcast_select_fusion), channel_id=1, source_target_pairs={{0,8},{1,5},{2,10},{3,7},{4,0},{5,13},{6,2},{7,15},{8,16},{9,1},{1... | collective-permute-start | bytes 393224 | tf_op jit(solution)/shard_map/ppermute | solution.py:29
  52.0 1.9 %collective-permute-start.14 = (bf16[256,128]{1,0:T(8,128)(2,1)S(1)}, bf16[256,128]{1,0:T(8,128)(2,1)S(1)}, u32[]{:S(2)}, u32[]{:S(2)}) collective-permute-start(bf16[256,128]{1,0:T(8,128)(2,1)S(1)} %get-tuple-element.14), channel_id=1, source_target_pairs={{0,1},{1,0},{2,3},{3,2},{4,5},{5,4},{6,7},{7,6},{8,9},{9,8},{10,11... | collective-permute-start | bytes 196616 | tf_op jit(solution)/shard_map/ppermute | solution.py:29
  52.1 4.5 %collective-permute-start.15 = (bf16[256,128]{1,0:T(8,128)(2,1)S(1)}, bf16[256,128]{1,0:T(8,128)(2,1)S(1)}, u32[]{:S(2)}, u32[]{:S(2)}) collective-permute-start(bf16[256,128]{1,0:T(8,128)(2,1)S(1)} %get-tuple-element.15), channel_id=1, source_target_pairs={{0,2},{1,3},{2,0},{3,1},{4,6},{5,7},{6,4},{7,5},{8,10},{9,11},{10,... | collective-permute-start | bytes 196616 | tf_op jit(solution)/shard_map/ppermute | solution.py:29
  53.6 4.1 %collective-permute-start.16 = (bf16[256,128]{1,0:T(8,128)(2,1)S(1)}, bf16[256,128]{1,0:T(8,128)(2,1)S(1)}, u32[]{:S(2)}, u32[]{:S(2)}) collective-permute-start(bf16[256,128]{1,0:T(8,128)(2,1)S(1)} %get-tuple-element.16), channel_id=1, source_target_pairs={{0,3},{1,2},{2,1},{3,0},{4,7},{5,6},{6,5},{7,4},{8,11},{9,10},{10,... | collective-permute-start | bytes 196616 | tf_op jit(solution)/shard_map/ppermute | solution.py:29
where the time goes:
time: 58.6 us; the launch traced here: 58.4 us
  waiting for transfers between devices  29.2 us (50%)
  starting transfers between devices  22.4 us (38%)
  matrix products  2.4 us (4%)
  other arithmetic  1.79 us (3%)
  local copies, waits for them, and re-layouts  1.45 us (2%)
  Pallas kernels  1.01 us (2%)
    ppermute x17, waiting for transfers between devices, move(): return lax.ppermute(value, AXES, pairs)  29.2 us
    ppermute x17, starting transfers between devices, move(): return lax.ppermute(value, AXES, pairs)  22.4 us
    dot_general x3, matrix products, product(): lax.dot_general(tile, dosage, (((0,), (1,)), ((), ())), preferred_element...  2.4 us
  transfers between devices with their start and end apart: 17, of which 9 were waited for; matrix products, arithmetic and copies ran while one was open for 5% of the time, Pallas kernels for 0%

commit v1 on v0

--- a/solution.py
+++ b/solution.py
@@ -24,8 +24,7 @@
     for place in range(loop_size):
         for part in range(seg_size):
             to = target(place, part)
-            if to is not None and 0 <= to[0] < loop_size:
-                pairs.append((place * seg_size + part, to[0] * seg_size + to[1]))
+            pairs.append((place * seg_size + part, to[0] * seg_size + to[1]))
     return lax.ppermute(value, AXES, pairs)
 
 
@@ -50,15 +49,22 @@
     odd, side = place % 2, part % 2
     half = block // 2
 
-    def masked_half(slot):
+    def masked_half(slot, inside):
         tile = lax.dynamic_slice(weight_tiles, (slot, side * half, 0), (1, half, genes))[0]
-        covered = (slot >= first_tile) & (slot <= last_tile)
+        covered = (slot >= first_tile) & (slot <= last_tile) & inside
         return jnp.where(covered[None, :], tile, jnp.zeros((), tile.dtype))
 
     far_slot = odd * (n_slots - 1)
-    far_half = masked_half(far_slot)
-    near_half = masked_half(n_slots - 1 - far_slot)
-    outward = lambda step: lambda l, s: (l + step if l % 2 else l - step, s)
+    far_half = masked_half(far_slot, (place > 0) & (place < loop_size - 1))
+    near_half = masked_half(n_slots - 1 - far_slot, True)
+
+    def outward(step):
+        def target(l, s):
+            to = l + step if l % 2 else l - step
+            return (to if 0 <= to < loop_size else (l if step == 1 else (l - 2) % loop_size if l % 2 == 0 else (l + 2) % loop_size), s)
+
+        return target
+
     partner = lambda l, s: (l ^ 1, s)
     sibling = lambda l, s: (l, s ^ 1)
 
@@ -77,11 +83,10 @@
     home_term = move(home_term, sizes, partner)
     far_term = term(far_half, move(far_half, sizes, sibling))
     near_half, _ = lax.optimization_barrier((near_half, far_term))
-    far_term = move(far_term, sizes, outward(2))
+    far_term = move(far_term.astype(jnp.bfloat16), sizes, outward(2))
     near_term = term(near_half, move(near_half, sizes, sibling))
     projection = (near_term + home_term + far_term).astype(jnp.bfloat16)
 
-    column = move(projection, sizes, partner)
     ahead = [ring_next(loop_size, l) for l in range(loop_size)]
     behind = [ahead.index(l) for l in range(loop_size)]
     blocks, sources = [projection], [list(range(loop_size))]
@@ -94,6 +99,11 @@
         back_from = [back_from[ahead[l]] for l in range(loop_size)]
         blocks += [forth, back]
         sources += [forth_from, back_from]
+    turns = [l for l in range(loop_size) if l ^ 1 in (ahead[l], behind[l])]
+    column = move(projection, sizes, lambda l, s: (l if l in turns else l ^ 1, s))
+    from_forth = functools.reduce(jnp.logical_or, [place == l for l in turns if behind[l] == l ^ 1])
+    from_back = functools.reduce(jnp.logical_or, [place == l for l in turns if ahead[l] == l ^ 1])
+    column = jnp.where(from_forth, blocks[1], jnp.where(from_back, blocks[2], column))
     opposite = jnp.where(side == 0, forth, back)
     blocks.append(move(opposite, sizes, lambda l, s: (behind[l] if s % 2 else ahead[l], s)))
     sources.append([forth_from[behind[l]] for l in range(loop_size)])

time: 58.6 us -> 55.7 us (0.951)
  waiting for transfers between devices: 29.2 us -> 25 us
  starting transfers between devices: 22.4 us -> 23.7 us
    ppermute x17, waiting for transfers between devices: 29.2 us -> 25 us  [move(): return lax.ppermute(value, AXES, pairs)]
    ppermute x17, starting transfers between devices: 22.4 us -> 23.7 us  [move(): return lax.ppermute(value, AXES, pairs)]
where the time goes in v1:
time: 55.7 us; the launch traced here: 55.4 us
  waiting for transfers between devices  25 us (45%)
  starting transfers between devices  23.7 us (43%)
  matrix products  2.4 us (4%)
  other arithmetic  1.8 us (3%)
  local copies, waits for them, and re-layouts  1.45 us (3%)
  Pallas kernels  1.01 us (2%)
    ppermute x17, waiting for transfers between devices, move(): return lax.ppermute(value, AXES, pairs)  25 us
    ppermute x17, starting transfers between devices, move(): return lax.ppermute(value, AXES, pairs)  23.7 us
    dot_general x3, matrix products, product(): lax.dot_general(tile, dosage, (((0,), (1,)), ((), ())), preferred_element...  2.4 us
  transfers between devices with their start and end apart: 17, of which 9 were waited for; matrix products, arithmetic and copies ran while one was open for 5% of the time, Pallas kernels for 0%

profile of v1, /device:TPU:0, one launch (start us, length us, event | category | flops | bytes accessed | tf_op | source)
XLA Modules:
  0.0 55.4 jit_solution(9371426257879148021)
XLA Ops:
  0.0 0.0 copy-start
  0.0 0.0 copy-start.1
  0.0 0.0 copy-start.2
  0.0 0.7 %copy-done.1 = s32[128]{0:T(128)S(1)} copy-done((s32[128]{0:T(128)S(1)}, s32[128]{0:T(128)}, u32[]{:S(2)}) %copy-start.1) | copy-done | bytes 536
  0.7 0.0 copy-done.2
  0.8 1.0 %bitcast_select_fusion = (bf16[512,128]{1,0:T(8,128)(2,1)S(1)}, bf16[512,128]{1,0:T(8,128)(2,1)S(1)}) fusion(bf16[3,1024,128]{2,1,0:T(8,128)(2,1)} %param.6, s32[]{:T(128)S(6)} %select_n.79, s32[]{:T(128)S(6)} %select_n.77, pred[128]{0:T(512)(128)(4,1)S(1)} %get-tuple-element.23, s32[]{:T(128)S(6)} %select_n.76, pred[128]{0:T(512)(128)(4,1)S(1)} %get-tuple-element.24), kind=kLoop, calls=%fused_computation.13 | loop fusion | flops 131072 | bytes 524556 | tf_op jit(solution)/shard_map/jit(_where)/select_n | solution.py:55
  1.8 0.7 %collective-permute-start.1 = (bf16[512,128]{1,0:T(8,128)(2,1)S(1)}, bf16[512,128]{1,0:T(8,128)(2,1)S(1)}, u32[]{:S(2)}, u32[]{:S(2)}) collective-permute-start(bf16[512,128]{1,0:T(8,128)(2,1)S(1)} %get-tuple-element.17), channel_id=1, source_target_pairs={{0,0},{1,1},{2,2},{3,3},{4,8},{5,9},{6,10},{7,11},{8,4},{9,5},{10,... | collective-permute-start | bytes 393224 | tf_op jit(solution)/shard_map/ppermute | solution.py:28
  2.5 0.0 copy-done
  2.5 1.4 %fusion.9 = f32[128,512]{1,0:T(8,128)S(1)} fusion(bf16[512,1024]{1,0:T(8,128)(2,1)S(1)} %copy-done, bf16[3,1024,128]{2,1,0:T(8,128)(2,1)} %param.6), kind=kOutput, calls=%fused_computation.10 | convolution fusion | flops 134217728 | bytes 1572864 | tf_op jit(solution)/shard_map/dot_general | solution.py:72
  3.9 0.0 collective-permute-done.1
  3.9 0.6 %collective-permute-start.2 = (bf16[512,128]{1,0:T(8,128)(2,1)S(1)}, bf16[512,128]{1,0:T(8,128)(2,1)S(1)}, u32[]{:S(2)}, u32[]{:S(2)}) collective-permute-start(bf16[512,128]{1,0:T(8,128)(2,1)S(1)} %collective-permute-done.1), channel_id=1, source_target_pairs={{0,1},{1,0},{2,3},{3,2},{4,5},{5,4},{6,7},{7,6},{8,9},{9,8},{10,11... | collective-permute-start | bytes 393224 | tf_op jit(solution)/shard_map/ppermute | solution.py:28
  4.5 8.3 %collective-permute-start = (bf16[512,128]{1,0:T(8,128)(2,1)S(1)}, bf16[512,128]{1,0:T(8,128)(2,1)S(1)}, u32[]{:S(2)}, u32[]{:S(2)}) collective-permute-start(bf16[512,128]{1,0:T(8,128)(2,1)S(1)} %get-tuple-element.18), channel_id=1, source_target_pairs={{0,4},{1,5},{2,6},{3,7},{4,0},{5,1},{6,2},{7,3},{8,12},{9,13},{10,... | collective-permute-start | bytes 393224 | tf_op jit(solution)/shard_map/ppermute | solution.py:28
  12.8 0.0 collective-permute-done.2
  12.9 0.5 fusion.2
  13.3 3.6 %collective-permute-done = bf16[512,128]{1,0:T(8,128)(2,1)S(1)} collective-permute-done((bf16[512,128]{1,0:T(8,128)(2,1)S(1)}, bf16[512,128]{1,0:T(8,128)(2,1)S(1)}, u32[]{:S(2)}, u32[]{:S(2)}) %collective-permute-start) | collective-permute-done | bytes 131104 | tf_op jit(solution)/shard_map/ppermute | solution.py:28
  17.0 0.0 collective-permute-start.3
  17.0 1.7 %collective-permute-start.4 = (f32[128,512]{1,0:T(8,128)S(1)}, f32[128,512]{1,0:T(8,128)S(1)}, u32[]{:S(2)}, u32[]{:S(2)}) collective-permute-start(f32[128,512]{1,0:T(8,128)S(1)} %fusion.9), channel_id=1, source_target_pairs={{0,4},{1,5},{2,6},{3,7},{4,0},{5,1},{6,2},{7,3},{8,12},{9,13},{10,... | collective-permute-start | bytes 786440 | tf_op jit(solution)/shard_map/ppermute | solution.py:28
  18.7 2.4 %collective-permute-start.5 = (bf16[128,512]{1,0:T(8,128)(2,1)S(1)}, bf16[128,512]{1,0:T(8,128)(2,1)S(1)}, u32[]{:S(2)}, u32[]{:S(2)}) collective-permute-start(bf16[128,512]{1,0:T(8,128)(2,1)S(1)} %fusion.2), channel_id=1, source_target_pairs={{0,24},{1,25},{2,26},{3,27},{4,12},{5,13},{6,14},{7,15},{8,0},{9,1... | collective-permute-start | bytes 393224 | tf_op jit(solution)/shard_map/ppermute | solution.py:28
  21.1 0.0 collective-permute-done.3
  21.1 4.6 %collective-permute-done.4 = f32[128,512]{1,0:T(8,128)S(1)} collective-permute-done((f32[128,512]{1,0:T(8,128)S(1)}, f32[128,512]{1,0:T(8,128)S(1)}, u32[]{:S(2)}, u32[]{:S(2)}) %collective-permute-start.4) | collective-permute-done | bytes 262176 | tf_op jit(solution)/shard_map/ppermute | solution.py:28
  25.7 0.0 collective-permute-done.5
  25.7 0.5 fusion.1.refs_0_
  26.2 1.8 %collective-permute-start.7 = (bf16[128,512]{1,0:T(8,128)(2,1)S(1)}, bf16[128,512]{1,0:T(8,128)(2,1)S(1)}, u32[]{:S(2)}, u32[]{:S(2)}) collective-permute-start(bf16[128,512]{1,0:T(8,128)(2,1)S(1)} %fusion.1.refs_0_), channel_id=1, source_target_pairs={{0,4},{1,5},{2,6},{3,7},{4,12},{5,13},{6,14},{7,15},{8,0},{9,1},{1... | collective-permute-start | bytes 393224 | tf_op jit(solution)/shard_map/ppermute | solution.py:28
  28.0 0.3 collective-permute-start.6
  28.3 3.1 %collective-permute-done.7.refs_2_ = bf16[128,512]{1,0:T(8,128)(2,1)S(1)} collective-permute-done((bf16[128,512]{1,0:T(8,128)(2,1)S(1)}, bf16[128,512]{1,0:T(8,128)(2,1)S(1)}, u32[]{:S(2)}, u32[]{:S(2)}) %collective-permute-start.7) | collective-permute-done | bytes 131104 | tf_op jit(solution)/shard_map/ppermute | solution.py:28
  31.4 1.7 %collective-permute-start.10 = (bf16[128,512]{1,0:T(8,128)(2,1)S(1)}, bf16[128,512]{1,0:T(8,128)(2,1)S(1)}, u32[]{:S(2)}, u32[]{:S(2)}) collective-permute-start(bf16[128,512]{1,0:T(8,128)(2,1)S(1)} %collective-permute-done.7.refs_2_), channel_id=1, source_target_pairs={{0,4},{1,5},{2,6},{3,7},{4,12},{5,13},{6,14},{7,15},{8,0},{9,1},{1... | collective-permute-start | bytes 393224 | tf_op jit(solution)/shard_map/ppermute | solution.py:28
  33.1 0.0 collective-permute-done.6.refs_1_
  33.1 0.3 collective-permute-start.9
  33.4 2.9 %collective-permute-done.10.refs_4_ = bf16[128,512]{1,0:T(8,128)(2,1)S(1)} collective-permute-done((bf16[128,512]{1,0:T(8,128)(2,1)S(1)}, bf16[128,512]{1,0:T(8,128)(2,1)S(1)}, u32[]{:S(2)}, u32[]{:S(2)}) %collective-permute-start.10) | collective-permute-done | bytes 131104 | tf_op jit(solution)/shard_map/ppermute | solution.py:28
  36.3 1.7 %collective-permute-start.12 = (bf16[128,512]{1,0:T(8,128)(2,1)S(1)}, bf16[128,512]{1,0:T(8,128)(2,1)S(1)}, u32[]{:S(2)}, u32[]{:S(2)}) collective-permute-start(bf16[128,512]{1,0:T(8,128)(2,1)S(1)} %collective-permute-done.10.refs_4_), channel_id=1, source_target_pairs={{0,4},{1,5},{2,6},{3,7},{4,12},{5,13},{6,14},{7,15},{8,0},{9,1},{1... | collective-permute-start | bytes 393224 | tf_op jit(solution)/shard_map/ppermute | solution.py:28
  38.0 0.0 collective-permute-done.9.refs_3_
  38.0 0.3 collective-permute-start.11
  38.4 0.7 %fusion.12.where_ref = s32[16]{0:T(128)S(1)} fusion(s32[32,16]{1,0:T(8,128)} %constant.51.clone, s32[]{:T(128)S(6)} %select_n.71), kind=kLoop, calls=%fused_computation.25 | loop fusion | bytes 132 | tf_op jit(solution)/shard_map/squeeze | solution.py:116
  39.1 0.7 %collective-permute-start.8 = (bf16[128,512]{1,0:T(8,128)(2,1)S(1)}, bf16[128,512]{1,0:T(8,128)(2,1)S(1)}, u32[]{:S(2)}, u32[]{:S(2)}) collective-permute-start(bf16[128,512]{1,0:T(8,128)(2,1)S(1)} %fusion.1.refs_0_), channel_id=1, source_target_pairs={{0,0},{1,1},{2,2},{3,3},{4,4},{5,5},{6,6},{7,7},{8,12},{9,13},{10,... | collective-permute-start | bytes 393224 | tf_op jit(solution)/shard_map/ppermute | solution.py:28
  39.7 1.6 %collective-permute-done.12.refs_6_ = bf16[128,512]{1,0:T(8,128)(2,1)S(1)} collective-permute-done((bf16[128,512]{1,0:T(8,128)(2,1)S(1)}, bf16[128,512]{1,0:T(8,128)(2,1)S(1)}, u32[]{:S(2)}, u32[]{:S(2)}) %collective-permute-start.12) | collective-permute-done | bytes 131104 | tf_op jit(solution)/shard_map/ppermute | solution.py:28
  41.3 1.7 %collective-permute-done.11.refs_5_ = bf16[128,512]{1,0:T(8,128)(2,1)S(1)} collective-permute-done((bf16[128,512]{1,0:T(8,128)(2,1)S(1)}, bf16[128,512]{1,0:T(8,128)(2,1)S(1)}, u32[]{:S(2)}, u32[]{:S(2)}) %collective-permute-start.11) | collective-permute-done | bytes 131104 | tf_op jit(solution)/shard_map/ppermute | solution.py:28
  43.0 1.3 %collective-permute-start.13 = (bf16[128,512]{1,0:T(8,128)(2,1)S(1)}, bf16[128,512]{1,0:T(8,128)(2,1)S(1)}, u32[]{:S(2)}, u32[]{:S(2)}) collective-permute-start(bf16[128,512]{1,0:T(8,128)(2,1)S(1)} %broadcast_select_fusion), channel_id=1, source_target_pairs={{0,8},{1,5},{2,10},{3,7},{4,0},{5,13},{6,2},{7,15},{8,16},{9,1},{1... | collective-permute-start | bytes 393224 | tf_op jit(solution)/shard_map/ppermute | solution.py:28
  44.3 0.0 collective-permute-done.8
  44.4 3.7 %collective-permute-done.13.refs_7_ = bf16[128,512]{1,0:T(8,128)(2,1)S(1)} collective-permute-done((bf16[128,512]{1,0:T(8,128)(2,1)S(1)}, bf16[128,512]{1,0:T(8,128)(2,1)S(1)}, u32[]{:S(2)}, u32[]{:S(2)}) %collective-permute-start.13) | collective-permute-done | bytes 131104 | tf_op jit(solution)/shard_map/ppermute | solution.py:28
  48.0 1.0 %pair_sums.1 = (f32[256,128]{1,0:T(8,128)S(1)}, bf16[256,128]{1,0:T(8,128)(2,1)S(1)}, bf16[256,128]{1,0:T(8,128)(2,1)S(1)}, bf16[256,128]{1,0:T(8,128)(2,1)S(1)}) custom-call(s32[16]{0:T(128)S(1)} %fusion.12.where_ref, bf16[128,512]{1,0:T(8,128)(2,1)S(1)} %select_select_fusion.column_ref, bf16[128,512]{1,0:T(8,128)(2,1)S(1)} %fusion.1.refs_0_, ...), custom_call_target="tpu_custom_call" | custom-call | tf_op jit(solution)/shard_map/pair_sums/pallas_call | solution.py:119
  49.1 0.1 collective-permute-start.14
  49.1 1.6 %collective-permute-start.15 = (bf16[256,128]{1,0:T(8,128)(2,1)S(1)}, bf16[256,128]{1,0:T(8,128)(2,1)S(1)}, u32[]{:S(2)}, u32[]{:S(2)}) collective-permute-start(bf16[256,128]{1,0:T(8,128)(2,1)S(1)} %get-tuple-element.15), channel_id=1, source_target_pairs={{0,2},{1,3},{2,0},{3,1},{4,6},{5,7},{6,4},{7,5},{8,10},{9,11},{10,... | collective-permute-start | bytes 196616 | tf_op jit(solution)/shard_map/ppermute | solution.py:28
  50.7 0.3 collective-permute-start.16
  51.0 0.0 collective-permute-done.14
  51.0 2.6 %collective-permute-done.15 = bf16[256,128]{1,0:T(8,128)(2,1)S(1)} collective-permute-done((bf16[256,128]{1,0:T(8,128)(2,1)S(1)}, bf16[256,128]{1,0:T(8,128)(2,1)S(1)}, u32[]{:S(2)}, u32[]{:S(2)}) %collective-permute-start.15) | collective-permute-done | bytes 65568 | tf_op jit(solution)/shard_map/ppermute | solution.py:28
  53.6 1.1 %collective-permute-done.16 = bf16[256,128]{1,0:T(8,128)(2,1)S(1)} collective-permute-done((bf16[256,128]{1,0:T(8,128)(2,1)S(1)}, bf16[256,128]{1,0:T(8,128)(2,1)S(1)}, u32[]{:S(2)}, u32[]{:S(2)}) %collective-permute-start.16) | collective-permute-done | bytes 65568 | tf_op jit(solution)/shard_map/ppermute | solution.py:28
  54.7 0.7 %add_multiply_fusion = f32[256,128]{1,0:T(8,128)} fusion(bf16[256,128]{1,0:T(8,128)(2,1)S(1)} %collective-permute-done.16, bf16[256,128]{1,0:T(8,128)(2,1)S(1)} %collective-permute-done.15, f32[256,128]{1,0:T(8,128)S(1)} %get-tuple-element.13, bf16[256,128]{1,0:T(8,128)(2,1)S(1)} %collective-permute-done.14), kind=kLoop, calls=%fused_computation.15 | loop fusion | flops 229376 | bytes 458752 | tf_op jit(solution)/shard_map/div | solution.py:131
  (5 shorter events, 0.1 us)
Async XLA Ops:
  0.0 2.5 %copy-start = (bf16[512,1024]{1,0:T(8,128)(2,1)S(1)}, bf16[512,1024]{1,0:T(8,128)(2,1)}, u32[]{:S(2)}) copy-start(bf16[512,1024]{1,0:T(8,128)(2,1)} %param.5) | copy-start | bytes 3145732
  0.0 0.7 %copy-start.1 = (s32[128]{0:T(128)S(1)}, s32[128]{0:T(128)}, u32[]{:S(2)}) copy-start(s32[128]{0:T(128)} %param.8) | copy-start | bytes 1540
  0.0 0.8 %copy-start.2 = (s32[128]{0:T(128)S(1)}, s32[128]{0:T(128)}, u32[]{:S(2)}) copy-start(s32[128]{0:T(128)} %param.7) | copy-start | bytes 1540
  1.8 2.1 %collective-permute-start.1 = (bf16[512,128]{1,0:T(8,128)(2,1)S(1)}, bf16[512,128]{1,0:T(8,128)(2,1)S(1)}, u32[]{:S(2)}, u32[]{:S(2)}) collective-permute-start(bf16[512,128]{1,0:T(8,128)(2,1)S(1)} %get-tuple-element.17), channel_id=1, source_target_pairs={{0,0},{1,1},{2,2},{3,3},{4,8},{5,9},{6,10},{7,11},{8,4},{9,5},{10,... | collective-permute-start | bytes 393224 | tf_op jit(solution)/shard_map/ppermute | solution.py:28
  3.9 8.9 %collective-permute-start.2 = (bf16[512,128]{1,0:T(8,128)(2,1)S(1)}, bf16[512,128]{1,0:T(8,128)(2,1)S(1)}, u32[]{:S(2)}, u32[]{:S(2)}) collective-permute-start(bf16[512,128]{1,0:T(8,128)(2,1)S(1)} %collective-permute-done.1), channel_id=1, source_target_pairs={{0,1},{1,0},{2,3},{3,2},{4,5},{5,4},{6,7},{7,6},{8,9},{9,8},{10,11... | collective-permute-start | bytes 393224 | tf_op jit(solution)/shard_map/ppermute | solution.py:28
  4.5 12.5 %collective-permute-start = (bf16[512,128]{1,0:T(8,128)(2,1)S(1)}, bf16[512,128]{1,0:T(8,128)(2,1)S(1)}, u32[]{:S(2)}, u32[]{:S(2)}) collective-permute-start(bf16[512,128]{1,0:T(8,128)(2,1)S(1)} %get-tuple-element.18), channel_id=1, source_target_pairs={{0,4},{1,5},{2,6},{3,7},{4,0},{5,1},{6,2},{7,3},{8,12},{9,13},{10,... | collective-permute-start | bytes 393224 | tf_op jit(solution)/shard_map/ppermute | solution.py:28
  17.0 4.1 %collective-permute-start.3 = (bf16[512,128]{1,0:T(8,128)(2,1)S(1)}, bf16[512,128]{1,0:T(8,128)(2,1)S(1)}, u32[]{:S(2)}, u32[]{:S(2)}) collective-permute-start(bf16[512,128]{1,0:T(8,128)(2,1)S(1)} %collective-permute-done), channel_id=1, source_target_pairs={{0,1},{1,0},{2,3},{3,2},{4,5},{5,4},{6,7},{7,6},{8,9},{9,8},{10,11... | collective-permute-start | bytes 393224 | tf_op jit(solution)/shard_map/ppermute | solution.py:28
  17.0 8.7 %collective-permute-start.4 = (f32[128,512]{1,0:T(8,128)S(1)}, f32[128,512]{1,0:T(8,128)S(1)}, u32[]{:S(2)}, u32[]{:S(2)}) collective-permute-start(f32[128,512]{1,0:T(8,128)S(1)} %fusion.9), channel_id=1, source_target_pairs={{0,4},{1,5},{2,6},{3,7},{4,0},{5,1},{6,2},{7,3},{8,12},{9,13},{10,... | collective-permute-start | bytes 786440 | tf_op jit(solution)/shard_map/ppermute | solution.py:28
  18.7 7.0 %collective-permute-start.5 = (bf16[128,512]{1,0:T(8,128)(2,1)S(1)}, bf16[128,512]{1,0:T(8,128)(2,1)S(1)}, u32[]{:S(2)}, u32[]{:S(2)}) collective-permute-start(bf16[128,512]{1,0:T(8,128)(2,1)S(1)} %fusion.2), channel_id=1, source_target_pairs={{0,24},{1,25},{2,26},{3,27},{4,12},{5,13},{6,14},{7,15},{8,0},{9,1... | collective-permute-start | bytes 393224 | tf_op jit(solution)/shard_map/ppermute | solution.py:28
  26.2 5.2 %collective-permute-start.7 = (bf16[128,512]{1,0:T(8,128)(2,1)S(1)}, bf16[128,512]{1,0:T(8,128)(2,1)S(1)}, u32[]{:S(2)}, u32[]{:S(2)}) collective-permute-start(bf16[128,512]{1,0:T(8,128)(2,1)S(1)} %fusion.1.refs_0_), channel_id=1, source_target_pairs={{0,4},{1,5},{2,6},{3,7},{4,12},{5,13},{6,14},{7,15},{8,0},{9,1},{1... | collective-permute-start | bytes 393224 | tf_op jit(solution)/shard_map/ppermute | solution.py:28
  28.0 5.1 %collective-permute-start.6 = (bf16[128,512]{1,0:T(8,128)(2,1)S(1)}, bf16[128,512]{1,0:T(8,128)(2,1)S(1)}, u32[]{:S(2)}, u32[]{:S(2)}) collective-permute-start(bf16[128,512]{1,0:T(8,128)(2,1)S(1)} %fusion.1.refs_0_), channel_id=1, source_target_pairs={{0,8},{1,9},{2,10},{3,11},{4,0},{5,1},{6,2},{7,3},{8,16},{9,17},{1... | collective-permute-start | bytes 393224 | tf_op jit(solution)/shard_map/ppermute | solution.py:28
  31.4 5.0 %collective-permute-start.10 = (bf16[128,512]{1,0:T(8,128)(2,1)S(1)}, bf16[128,512]{1,0:T(8,128)(2,1)S(1)}, u32[]{:S(2)}, u32[]{:S(2)}) collective-permute-start(bf16[128,512]{1,0:T(8,128)(2,1)S(1)} %collective-permute-done.7.refs_2_), channel_id=1, source_target_pairs={{0,4},{1,5},{2,6},{3,7},{4,12},{5,13},{6,14},{7,15},{8,0},{9,1},{1... | collective-permute-start | bytes 393224 | tf_op jit(solution)/shard_map/ppermute | solution.py:28
  33.1 5.0 %collective-permute-start.9 = (bf16[128,512]{1,0:T(8,128)(2,1)S(1)}, bf16[128,512]{1,0:T(8,128)(2,1)S(1)}, u32[]{:S(2)}, u32[]{:S(2)}) collective-permute-start(bf16[128,512]{1,0:T(8,128)(2,1)S(1)} %collective-permute-done.6.refs_1_), channel_id=1, source_target_pairs={{0,8},{1,9},{2,10},{3,11},{4,0},{5,1},{6,2},{7,3},{8,16},{9,17},{1... | collective-permute-start | bytes 393224 | tf_op jit(solution)/shard_map/ppermute | solution.py:28
  36.3 5.0 %collective-permute-start.12 = (bf16[128,512]{1,0:T(8,128)(2,1)S(1)}, bf16[128,512]{1,0:T(8,128)(2,1)S(1)}, u32[]{:S(2)}, u32[]{:S(2)}) collective-permute-start(bf16[128,512]{1,0:T(8,128)(2,1)S(1)} %collective-permute-done.10.refs_4_), channel_id=1, source_target_pairs={{0,4},{1,5},{2,6},{3,7},{4,12},{5,13},{6,14},{7,15},{8,0},{9,1},{1... | collective-permute-start | bytes 393224 | tf_op jit(solution)/shard_map/ppermute | solution.py:28
  38.0 5.0 %collective-permute-start.11 = (bf16[128,512]{1,0:T(8,128)(2,1)S(1)}, bf16[128,512]{1,0:T(8,128)(2,1)S(1)}, u32[]{:S(2)}, u32[]{:S(2)}) collective-permute-start(bf16[128,512]{1,0:T(8,128)(2,1)S(1)} %collective-permute-done.9.refs_3_), channel_id=1, source_target_pairs={{0,8},{1,9},{2,10},{3,11},{4,0},{5,1},{6,2},{7,3},{8,16},{9,17},{1... | collective-permute-start | bytes 393224 | tf_op jit(solution)/shard_map/ppermute | solution.py:28
  39.1 5.3 %collective-permute-start.8 = (bf16[128,512]{1,0:T(8,128)(2,1)S(1)}, bf16[128,512]{1,0:T(8,128)(2,1)S(1)}, u32[]{:S(2)}, u32[]{:S(2)}) collective-permute-start(bf16[128,512]{1,0:T(8,128)(2,1)S(1)} %fusion.1.refs_0_), channel_id=1, source_target_pairs={{0,0},{1,1},{2,2},{3,3},{4,4},{5,5},{6,6},{7,7},{8,12},{9,13},{10,... | collective-permute-start | bytes 393224 | tf_op jit(solution)/shard_map/ppermute | solution.py:28
  43.0 5.0 %collective-permute-start.13 = (bf16[128,512]{1,0:T(8,128)(2,1)S(1)}, bf16[128,512]{1,0:T(8,128)(2,1)S(1)}, u32[]{:S(2)}, u32[]{:S(2)}) collective-permute-start(bf16[128,512]{1,0:T(8,128)(2,1)S(1)} %broadcast_select_fusion), channel_id=1, source_target_pairs={{0,8},{1,5},{2,10},{3,7},{4,0},{5,13},{6,2},{7,15},{8,16},{9,1},{1... | collective-permute-start | bytes 393224 | tf_op jit(solution)/shard_map/ppermute | solution.py:28
  49.1 1.9 %collective-permute-start.14 = (bf16[256,128]{1,0:T(8,128)(2,1)S(1)}, bf16[256,128]{1,0:T(8,128)(2,1)S(1)}, u32[]{:S(2)}, u32[]{:S(2)}) collective-permute-start(bf16[256,128]{1,0:T(8,128)(2,1)S(1)} %get-tuple-element.14), channel_id=1, source_target_pairs={{0,1},{1,0},{2,3},{3,2},{4,5},{5,4},{6,7},{7,6},{8,9},{9,8},{10,11... | collective-permute-start | bytes 196616 | tf_op jit(solution)/shard_map/ppermute | solution.py:28
  49.1 4.5 %collective-permute-start.15 = (bf16[256,128]{1,0:T(8,128)(2,1)S(1)}, bf16[256,128]{1,0:T(8,128)(2,1)S(1)}, u32[]{:S(2)}, u32[]{:S(2)}) collective-permute-start(bf16[256,128]{1,0:T(8,128)(2,1)S(1)} %get-tuple-element.15), channel_id=1, source_target_pairs={{0,2},{1,3},{2,0},{3,1},{4,6},{5,7},{6,4},{7,5},{8,10},{9,11},{10,... | collective-permute-start | bytes 196616 | tf_op jit(solution)/shard_map/ppermute | solution.py:28
  50.7 4.1 %collective-permute-start.16 = (bf16[256,128]{1,0:T(8,128)(2,1)S(1)}, bf16[256,128]{1,0:T(8,128)(2,1)S(1)}, u32[]{:S(2)}, u32[]{:S(2)}) collective-permute-start(bf16[256,128]{1,0:T(8,128)(2,1)S(1)} %get-tuple-element.16), channel_id=1, source_target_pairs={{0,3},{1,2},{2,1},{3,0},{4,7},{5,6},{6,5},{7,4},{8,11},{9,10},{10,... | collective-permute-start | bytes 196616 | tf_op jit(solution)/shard_map/ppermute | solution.py:28

commit v2 on v1

--- a/solution.py
+++ b/solution.py
@@ -28,9 +28,16 @@
     return lax.ppermute(value, AXES, pairs)
 
 
-def pair_kernel(n_blocks, where_ref, column_ref, *refs):
-    blocks, own_ref, away_refs, sums_ref = refs[:n_blocks], refs[n_blocks], refs[n_blocks + 1 : -1], refs[-1]
+def pair_kernel(n_blocks, where_ref, *refs):
+    blocks, own_ref, away_refs = refs[:n_blocks], refs[n_blocks], refs[n_blocks + 1 : -2]
+    column_ref, sums_ref = refs[-2:]
     genes = column_ref.shape[0]
+    for k, block in enumerate(blocks):
+
+        @pl.when(where_ref[2 * n_blocks] == k)
+        def _():
+            column_ref[...] = block[...]
+
     column = column_ref[...]
     for k, block in enumerate(blocks):
         product = lax.dot_general(block[...], column, (((1,), (1,)), ((), ())), preferred_element_type=jnp.float32)
@@ -99,32 +106,28 @@
         back_from = [back_from[ahead[l]] for l in range(loop_size)]
         blocks += [forth, back]
         sources += [forth_from, back_from]
-    turns = [l for l in range(loop_size) if l ^ 1 in (ahead[l], behind[l])]
-    column = move(projection, sizes, lambda l, s: (l if l in turns else l ^ 1, s))
-    from_forth = functools.reduce(jnp.logical_or, [place == l for l in turns if behind[l] == l ^ 1])
-    from_back = functools.reduce(jnp.logical_or, [place == l for l in turns if ahead[l] == l ^ 1])
-    column = jnp.where(from_forth, blocks[1], jnp.where(from_back, blocks[2], column))
-    opposite = jnp.where(side == 0, forth, back)
-    blocks.append(move(opposite, sizes, lambda l, s: (behind[l] if s % 2 else ahead[l], s)))
+    blocks.append(move(forth, sizes, lambda l, s: (ahead[l], s)))
     sources.append([forth_from[behind[l]] for l in range(loop_size)])
 
     per_chunk = loop_size // seg_size
     held = np.array(sources).T ^ 1
     parts = np.arange(seg_size)[None, :, None]
     table = np.stack([(held[:, None, :] // per_chunk) ^ parts, np.broadcast_to((held % per_chunk)[:, None, :], (loop_size, seg_size, loop_size))], axis=-1)
-    table = jnp.asarray(table.reshape(loop_size * seg_size, -1), jnp.int32)
+    table = table.reshape(loop_size * seg_size, 2 * loop_size)
+    own_genes = np.argmax(held == np.arange(loop_size)[:, None], axis=1)
+    table = jnp.asarray(np.concatenate([table, np.repeat(own_genes, seg_size)[:, None]], axis=1), jnp.int32)
     where = lax.dynamic_slice(table, (place * seg_size + part, 0), (1, table.shape[1]))[0]
     rows = loop_size * genes // seg_size
     vmem = pl.BlockSpec(memory_space=pltpu.VMEM)
     own, *away = pl.pallas_call(
         functools.partial(pair_kernel, loop_size),
         out_shape=[jax.ShapeDtypeStruct((rows, genes), jnp.float32)] + [jax.ShapeDtypeStruct((rows, genes), jnp.bfloat16)] * (seg_size - 1),
-        in_specs=[pl.BlockSpec(memory_space=pltpu.SMEM)] + [vmem] * (loop_size + 1),
+        in_specs=[pl.BlockSpec(memory_space=pltpu.SMEM)] + [vmem] * loop_size,
         out_specs=[vmem] * seg_size,
-        scratch_shapes=[pltpu.VMEM((seg_size, rows, genes), jnp.float32)],
+        scratch_shapes=[pltpu.VMEM((genes, samples), jnp.bfloat16), pltpu.VMEM((seg_size, rows, genes), jnp.float32)],
         compiler_params=pltpu.CompilerParams(vmem_limit_bytes=2 * (loop_size + 1) * genes * samples * 2 + 3 * seg_size * rows * genes * 4),
         name="pair_sums",
-    )(where, column, *blocks)
+    )(where, *blocks)
     total = own
     for j in range(1, seg_size):
         total = total + move(away[j - 1], sizes, lambda l, s: (l, s ^ j)).astype(jnp.float32)

time: 55.7 us -> 54.5 us (0.978)
  waiting for transfers between devices: 25 us -> 24 us
    ppermute x17 -> x16, waiting for transfers between devices: 25 us -> 24 us  [move(): return lax.ppermute(value, AXES, pairs)]
    ppermute x17 -> x16, starting transfers between devices: 23.7 us -> 23.6 us  [move(): return lax.ppermute(value, AXES, pairs)]
  transfers between devices with their start and end apart: 17 -> 16, of which waited for: 9 -> 8; matrix products, arithmetic and copies ran while one was open for 5% -> 5% of each run, Pallas kernels for 0% -> 0%
where the time goes in v2:
time: 54.5 us; the launch traced here: 54.3 us
  waiting for transfers between devices  24 us (44%)
  starting transfers between devices  23.6 us (43%)
  matrix products  2.4 us (4%)
  other arithmetic  1.76 us (3%)
  local copies, waits for them, and re-layouts  1.45 us (3%)
  Pallas kernels  1.08 us (2%)
    ppermute x16, waiting for transfers between devices, move(): return lax.ppermute(value, AXES, pairs)  24 us
    ppermute x16, starting transfers between devices, move(): return lax.ppermute(value, AXES, pairs)  23.6 us
    dot_general x3, matrix products, product(): lax.dot_general(tile, dosage, (((0,), (1,)), ((), ())), preferred_element...  2.4 us
  transfers between devices with their start and end apart: 16, of which 8 were waited for; matrix products, arithmetic and copies ran while one was open for 5% of the time, Pallas kernels for 0%

profile of v2, /device:TPU:0, one launch (start us, length us, event | category | flops | bytes accessed | tf_op | source)
XLA Modules:
  0.0 54.3 jit_solution(3747648864001728320)
XLA Ops:
  0.0 0.0 copy-start
  0.0 0.0 copy-start.1
  0.0 0.0 copy-start.2
  0.0 0.7 %copy-done.1 = s32[128]{0:T(128)S(1)} copy-done((s32[128]{0:T(128)S(1)}, s32[128]{0:T(128)}, u32[]{:S(2)}) %copy-start.1) | copy-done | bytes 536
  0.7 0.0 copy-done.2
  0.8 1.0 %bitcast_select_fusion = (bf16[512,128]{1,0:T(8,128)(2,1)S(1)}, bf16[512,128]{1,0:T(8,128)(2,1)S(1)}) fusion(bf16[3,1024,128]{2,1,0:T(8,128)(2,1)} %param.6, s32[]{:T(128)S(6)} %select_n.58, s32[]{:T(128)S(6)} %select_n.56, pred[128]{0:T(512)(128)(4,1)S(1)} %get-tuple-element.23, s32[]{:T(128)S(6)} %select_n.55, pred[128]{0:T(512)(128)(4,1)S(1)} %get-tuple-element.24), kind=kLoop, calls=%fused_computation.13 | loop fusion | flops 131072 | bytes 524556 | tf_op jit(solution)/shard_map/jit(_where)/select_n | solution.py:62
  1.8 0.7 %collective-permute-start.1 = (bf16[512,128]{1,0:T(8,128)(2,1)S(1)}, bf16[512,128]{1,0:T(8,128)(2,1)S(1)}, u32[]{:S(2)}, u32[]{:S(2)}) collective-permute-start(bf16[512,128]{1,0:T(8,128)(2,1)S(1)} %get-tuple-element.17), channel_id=1, source_target_pairs={{0,0},{1,1},{2,2},{3,3},{4,8},{5,9},{6,10},{7,11},{8,4},{9,5},{10,... | collective-permute-start | bytes 393224 | tf_op jit(solution)/shard_map/ppermute | solution.py:28
  2.5 0.0 copy-done
  2.5 1.4 %fusion.9 = f32[128,512]{1,0:T(8,128)S(1)} fusion(bf16[512,1024]{1,0:T(8,128)(2,1)S(1)} %copy-done, bf16[3,1024,128]{2,1,0:T(8,128)(2,1)} %param.6), kind=kOutput, calls=%fused_computation.10 | convolution fusion | flops 134217728 | bytes 1572864 | tf_op jit(solution)/shard_map/dot_general | solution.py:79
  3.9 0.0 collective-permute-done.1
  3.9 0.6 %collective-permute-start.2 = (bf16[512,128]{1,0:T(8,128)(2,1)S(1)}, bf16[512,128]{1,0:T(8,128)(2,1)S(1)}, u32[]{:S(2)}, u32[]{:S(2)}) collective-permute-start(bf16[512,128]{1,0:T(8,128)(2,1)S(1)} %collective-permute-done.1), channel_id=1, source_target_pairs={{0,1},{1,0},{2,3},{3,2},{4,5},{5,4},{6,7},{7,6},{8,9},{9,8},{10,11... | collective-permute-start | bytes 393224 | tf_op jit(solution)/shard_map/ppermute | solution.py:28
  4.5 8.3 %collective-permute-start = (bf16[512,128]{1,0:T(8,128)(2,1)S(1)}, bf16[512,128]{1,0:T(8,128)(2,1)S(1)}, u32[]{:S(2)}, u32[]{:S(2)}) collective-permute-start(bf16[512,128]{1,0:T(8,128)(2,1)S(1)} %get-tuple-element.18), channel_id=1, source_target_pairs={{0,4},{1,5},{2,6},{3,7},{4,0},{5,1},{6,2},{7,3},{8,12},{9,13},{10,... | collective-permute-start | bytes 393224 | tf_op jit(solution)/shard_map/ppermute | solution.py:28
  12.8 0.0 collective-permute-done.2
  12.9 0.5 fusion.2
  13.3 3.6 %collective-permute-done = bf16[512,128]{1,0:T(8,128)(2,1)S(1)} collective-permute-done((bf16[512,128]{1,0:T(8,128)(2,1)S(1)}, bf16[512,128]{1,0:T(8,128)(2,1)S(1)}, u32[]{:S(2)}, u32[]{:S(2)}) %collective-permute-start) | collective-permute-done | bytes 131104 | tf_op jit(solution)/shard_map/ppermute | solution.py:28
  17.0 0.0 collective-permute-start.3
  17.0 1.7 %collective-permute-start.4 = (f32[128,512]{1,0:T(8,128)S(1)}, f32[128,512]{1,0:T(8,128)S(1)}, u32[]{:S(2)}, u32[]{:S(2)}) collective-permute-start(f32[128,512]{1,0:T(8,128)S(1)} %fusion.9), channel_id=1, source_target_pairs={{0,4},{1,5},{2,6},{3,7},{4,0},{5,1},{6,2},{7,3},{8,12},{9,13},{10,... | collective-permute-start | bytes 786440 | tf_op jit(solution)/shard_map/ppermute | solution.py:28
  18.7 2.4 %collective-permute-start.5 = (bf16[128,512]{1,0:T(8,128)(2,1)S(1)}, bf16[128,512]{1,0:T(8,128)(2,1)S(1)}, u32[]{:S(2)}, u32[]{:S(2)}) collective-permute-start(bf16[128,512]{1,0:T(8,128)(2,1)S(1)} %fusion.2), channel_id=1, source_target_pairs={{0,24},{1,25},{2,26},{3,27},{4,12},{5,13},{6,14},{7,15},{8,0},{9,1... | collective-permute-start | bytes 393224 | tf_op jit(solution)/shard_map/ppermute | solution.py:28
  21.1 0.0 collective-permute-done.3
  21.1 4.6 %collective-permute-done.4 = f32[128,512]{1,0:T(8,128)S(1)} collective-permute-done((f32[128,512]{1,0:T(8,128)S(1)}, f32[128,512]{1,0:T(8,128)S(1)}, u32[]{:S(2)}, u32[]{:S(2)}) %collective-permute-start.4) | collective-permute-done | bytes 262176 | tf_op jit(solution)/shard_map/ppermute | solution.py:28
  25.7 0.0 collective-permute-done.5
  25.7 0.5 fusion.1.refs_0_
  26.2 1.9 %collective-permute-start.6 = (bf16[128,512]{1,0:T(8,128)(2,1)S(1)}, bf16[128,512]{1,0:T(8,128)(2,1)S(1)}, u32[]{:S(2)}, u32[]{:S(2)}) collective-permute-start(bf16[128,512]{1,0:T(8,128)(2,1)S(1)} %fusion.1.refs_0_), channel_id=1, source_target_pairs={{0,8},{1,9},{2,10},{3,11},{4,0},{5,1},{6,2},{7,3},{8,16},{9,17},{1... | collective-permute-start | bytes 393224 | tf_op jit(solution)/shard_map/ppermute | solution.py:28
  28.1 0.2 collective-permute-start.7
  28.3 3.0 %collective-permute-done.6.refs_1_ = bf16[128,512]{1,0:T(8,128)(2,1)S(1)} collective-permute-done((bf16[128,512]{1,0:T(8,128)(2,1)S(1)}, bf16[128,512]{1,0:T(8,128)(2,1)S(1)}, u32[]{:S(2)}, u32[]{:S(2)}) %collective-permute-start.6) | collective-permute-done | bytes 131104 | tf_op jit(solution)/shard_map/ppermute | solution.py:28
  31.3 1.8 %collective-permute-start.8 = (bf16[128,512]{1,0:T(8,128)(2,1)S(1)}, bf16[128,512]{1,0:T(8,128)(2,1)S(1)}, u32[]{:S(2)}, u32[]{:S(2)}) collective-permute-start(bf16[128,512]{1,0:T(8,128)(2,1)S(1)} %collective-permute-done.6.refs_1_), channel_id=1, source_target_pairs={{0,8},{1,9},{2,10},{3,11},{4,0},{5,1},{6,2},{7,3},{8,16},{9,17},{1... | collective-permute-start | bytes 393224 | tf_op jit(solution)/shard_map/ppermute | solution.py:28
  33.1 0.0 collective-permute-done.7.refs_2_
  33.1 0.2 collective-permute-start.9
  33.3 2.9 %collective-permute-done.8.refs_3_ = bf16[128,512]{1,0:T(8,128)(2,1)S(1)} collective-permute-done((bf16[128,512]{1,0:T(8,128)(2,1)S(1)}, bf16[128,512]{1,0:T(8,128)(2,1)S(1)}, u32[]{:S(2)}, u32[]{:S(2)}) %collective-permute-start.8) | collective-permute-done | bytes 131104 | tf_op jit(solution)/shard_map/ppermute | solution.py:28
  36.3 1.8 %collective-permute-start.10 = (bf16[128,512]{1,0:T(8,128)(2,1)S(1)}, bf16[128,512]{1,0:T(8,128)(2,1)S(1)}, u32[]{:S(2)}, u32[]{:S(2)}) collective-permute-start(bf16[128,512]{1,0:T(8,128)(2,1)S(1)} %collective-permute-done.8.refs_3_), channel_id=1, source_target_pairs={{0,8},{1,9},{2,10},{3,11},{4,0},{5,1},{6,2},{7,3},{8,16},{9,17},{1... | collective-permute-start | bytes 393224 | tf_op jit(solution)/shard_map/ppermute | solution.py:28
  38.1 0.0 collective-permute-done.9.refs_4_
  38.1 0.2 collective-permute-start.11
  38.3 3.5 %collective-permute-done.10.refs_5_ = bf16[128,512]{1,0:T(8,128)(2,1)S(1)} collective-permute-done((bf16[128,512]{1,0:T(8,128)(2,1)S(1)}, bf16[128,512]{1,0:T(8,128)(2,1)S(1)}, u32[]{:S(2)}, u32[]{:S(2)}) %collective-permute-start.10) | collective-permute-done | bytes 131104 | tf_op jit(solution)/shard_map/ppermute | solution.py:28
  41.9 1.9 %collective-permute-start.12 = (bf16[128,512]{1,0:T(8,128)(2,1)S(1)}, bf16[128,512]{1,0:T(8,128)(2,1)S(1)}, u32[]{:S(2)}, u32[]{:S(2)}) collective-permute-start(bf16[128,512]{1,0:T(8,128)(2,1)S(1)} %collective-permute-done.10.refs_5_), channel_id=1, source_target_pairs={{0,8},{1,9},{2,10},{3,11},{4,0},{5,1},{6,2},{7,3},{8,16},{9,17},{1... | collective-permute-start | bytes 393224 | tf_op jit(solution)/shard_map/ppermute | solution.py:28
  43.7 0.7 %fusion.12.where_ref = s32[17]{0:T(128)S(1)} fusion(s32[32,17]{1,0:T(8,128)} %constant.48.clone, s32[]{:T(128)S(6)} %select_n.51), kind=kLoop, calls=%fused_computation.23 | loop fusion | bytes 140 | tf_op jit(solution)/shard_map/squeeze | solution.py:119
  44.4 0.0 collective-permute-done.11.refs_6_
  44.4 2.4 %collective-permute-done.12.refs_7_ = bf16[128,512]{1,0:T(8,128)(2,1)S(1)} collective-permute-done((bf16[128,512]{1,0:T(8,128)(2,1)S(1)}, bf16[128,512]{1,0:T(8,128)(2,1)S(1)}, u32[]{:S(2)}, u32[]{:S(2)}) %collective-permute-start.12) | collective-permute-done | bytes 131104 | tf_op jit(solution)/shard_map/ppermute | solution.py:28
  46.9 1.1 %pair_sums.1 = (f32[256,128]{1,0:T(8,128)S(1)}, bf16[256,128]{1,0:T(8,128)(2,1)S(1)}, bf16[256,128]{1,0:T(8,128)(2,1)S(1)}, bf16[256,128]{1,0:T(8,128)(2,1)S(1)}) custom-call(s32[17]{0:T(128)S(1)} %fusion.12.where_ref, bf16[128,512]{1,0:T(8,128)(2,1)S(1)} %fusion.1.refs_0_, bf16[128,512]{1,0:T(8,128)(2,1)S(1)} %collective-permute-done.6.refs_1_, ...), custom_call_target="tpu_custom_call" | custom-call | tf_op jit(solution)/shard_map/pair_sums/pallas_call | solution.py:122
  47.9 0.1 collective-permute-start.13
  48.0 1.6 %collective-permute-start.14 = (bf16[256,128]{1,0:T(8,128)(2,1)S(1)}, bf16[256,128]{1,0:T(8,128)(2,1)S(1)}, u32[]{:S(2)}, u32[]{:S(2)}) collective-permute-start(bf16[256,128]{1,0:T(8,128)(2,1)S(1)} %get-tuple-element.15), channel_id=1, source_target_pairs={{0,2},{1,3},{2,0},{3,1},{4,6},{5,7},{6,4},{7,5},{8,10},{9,11},{10,... | collective-permute-start | bytes 196616 | tf_op jit(solution)/shard_map/ppermute | solution.py:28
  49.6 0.3 collective-permute-start.15
  49.9 0.0 collective-permute-done.13
  49.9 2.6 %collective-permute-done.14 = bf16[256,128]{1,0:T(8,128)(2,1)S(1)} collective-permute-done((bf16[256,128]{1,0:T(8,128)(2,1)S(1)}, bf16[256,128]{1,0:T(8,128)(2,1)S(1)}, u32[]{:S(2)}, u32[]{:S(2)}) %collective-permute-start.14) | collective-permute-done | bytes 65568 | tf_op jit(solution)/shard_map/ppermute | solution.py:28
  52.5 1.1 %collective-permute-done.15 = bf16[256,128]{1,0:T(8,128)(2,1)S(1)} collective-permute-done((bf16[256,128]{1,0:T(8,128)(2,1)S(1)}, bf16[256,128]{1,0:T(8,128)(2,1)S(1)}, u32[]{:S(2)}, u32[]{:S(2)}) %collective-permute-start.15) | collective-permute-done | bytes 65568 | tf_op jit(solution)/shard_map/ppermute | solution.py:28
  53.6 0.7 %add_multiply_fusion = f32[256,128]{1,0:T(8,128)} fusion(bf16[256,128]{1,0:T(8,128)(2,1)S(1)} %collective-permute-done.15, bf16[256,128]{1,0:T(8,128)(2,1)S(1)} %collective-permute-done.14, f32[256,128]{1,0:T(8,128)S(1)} %get-tuple-element.13, bf16[256,128]{1,0:T(8,128)(2,1)S(1)} %collective-permute-done.13), kind=kLoop, calls=%fused_computation.15 | loop fusion | flops 229376 | bytes 458752 | tf_op jit(solution)/shard_map/div | solution.py:134
  (3 shorter events, 0.1 us)
Async XLA Ops:
  0.0 2.5 %copy-start = (bf16[512,1024]{1,0:T(8,128)(2,1)S(1)}, bf16[512,1024]{1,0:T(8,128)(2,1)}, u32[]{:S(2)}) copy-start(bf16[512,1024]{1,0:T(8,128)(2,1)} %param.5) | copy-start | bytes 3145732
  0.0 0.7 %copy-start.1 = (s32[128]{0:T(128)S(1)}, s32[128]{0:T(128)}, u32[]{:S(2)}) copy-start(s32[128]{0:T(128)} %param.8) | copy-start | bytes 1540
  0.0 0.8 %copy-start.2 = (s32[128]{0:T(128)S(1)}, s32[128]{0:T(128)}, u32[]{:S(2)}) copy-start(s32[128]{0:T(128)} %param.7) | copy-start | bytes 1540
  1.8 2.1 %collective-permute-start.1 = (bf16[512,128]{1,0:T(8,128)(2,1)S(1)}, bf16[512,128]{1,0:T(8,128)(2,1)S(1)}, u32[]{:S(2)}, u32[]{:S(2)}) collective-permute-start(bf16[512,128]{1,0:T(8,128)(2,1)S(1)} %get-tuple-element.17), channel_id=1, source_target_pairs={{0,0},{1,1},{2,2},{3,3},{4,8},{5,9},{6,10},{7,11},{8,4},{9,5},{10,... | collective-permute-start | bytes 393224 | tf_op jit(solution)/shard_map/ppermute | solution.py:28
  3.9 8.9 %collective-permute-start.2 = (bf16[512,128]{1,0:T(8,128)(2,1)S(1)}, bf16[512,128]{1,0:T(8,128)(2,1)S(1)}, u32[]{:S(2)}, u32[]{:S(2)}) collective-permute-start(bf16[512,128]{1,0:T(8,128)(2,1)S(1)} %collective-permute-done.1), channel_id=1, source_target_pairs={{0,1},{1,0},{2,3},{3,2},{4,5},{5,4},{6,7},{7,6},{8,9},{9,8},{10,11... | collective-permute-start | bytes 393224 | tf_op jit(solution)/shard_map/ppermute | solution.py:28
  4.5 12.5 %collective-permute-start = (bf16[512,128]{1,0:T(8,128)(2,1)S(1)}, bf16[512,128]{1,0:T(8,128)(2,1)S(1)}, u32[]{:S(2)}, u32[]{:S(2)}) collective-permute-start(bf16[512,128]{1,0:T(8,128)(2,1)S(1)} %get-tuple-element.18), channel_id=1, source_target_pairs={{0,4},{1,5},{2,6},{3,7},{4,0},{5,1},{6,2},{7,3},{8,12},{9,13},{10,... | collective-permute-start | bytes 393224 | tf_op jit(solution)/shard_map/ppermute | solution.py:28
  17.0 4.1 %collective-permute-start.3 = (bf16[512,128]{1,0:T(8,128)(2,1)S(1)}, bf16[512,128]{1,0:T(8,128)(2,1)S(1)}, u32[]{:S(2)}, u32[]{:S(2)}) collective-permute-start(bf16[512,128]{1,0:T(8,128)(2,1)S(1)} %collective-permute-done), channel_id=1, source_target_pairs={{0,1},{1,0},{2,3},{3,2},{4,5},{5,4},{6,7},{7,6},{8,9},{9,8},{10,11... | collective-permute-start | bytes 393224 | tf_op jit(solution)/shard_map/ppermute | solution.py:28
  17.0 8.7 %collective-permute-start.4 = (f32[128,512]{1,0:T(8,128)S(1)}, f32[128,512]{1,0:T(8,128)S(1)}, u32[]{:S(2)}, u32[]{:S(2)}) collective-permute-start(f32[128,512]{1,0:T(8,128)S(1)} %fusion.9), channel_id=1, source_target_pairs={{0,4},{1,5},{2,6},{3,7},{4,0},{5,1},{6,2},{7,3},{8,12},{9,13},{10,... | collective-permute-start | bytes 786440 | tf_op jit(solution)/shard_map/ppermute | solution.py:28
  18.7 7.0 %collective-permute-start.5 = (bf16[128,512]{1,0:T(8,128)(2,1)S(1)}, bf16[128,512]{1,0:T(8,128)(2,1)S(1)}, u32[]{:S(2)}, u32[]{:S(2)}) collective-permute-start(bf16[128,512]{1,0:T(8,128)(2,1)S(1)} %fusion.2), channel_id=1, source_target_pairs={{0,24},{1,25},{2,26},{3,27},{4,12},{5,13},{6,14},{7,15},{8,0},{9,1... | collective-permute-start | bytes 393224 | tf_op jit(solution)/shard_map/ppermute | solution.py:28
  26.2 5.1 %collective-permute-start.6 = (bf16[128,512]{1,0:T(8,128)(2,1)S(1)}, bf16[128,512]{1,0:T(8,128)(2,1)S(1)}, u32[]{:S(2)}, u32[]{:S(2)}) collective-permute-start(bf16[128,512]{1,0:T(8,128)(2,1)S(1)} %fusion.1.refs_0_), channel_id=1, source_target_pairs={{0,8},{1,9},{2,10},{3,11},{4,0},{5,1},{6,2},{7,3},{8,16},{9,17},{1... | collective-permute-start | bytes 393224 | tf_op jit(solution)/shard_map/ppermute | solution.py:28
  28.1 5.0 %collective-permute-start.7 = (bf16[128,512]{1,0:T(8,128)(2,1)S(1)}, bf16[128,512]{1,0:T(8,128)(2,1)S(1)}, u32[]{:S(2)}, u32[]{:S(2)}) collective-permute-start(bf16[128,512]{1,0:T(8,128)(2,1)S(1)} %fusion.1.refs_0_), channel_id=1, source_target_pairs={{0,4},{1,5},{2,6},{3,7},{4,12},{5,13},{6,14},{7,15},{8,0},{9,1},{1... | collective-permute-start | bytes 393224 | tf_op jit(solution)/shard_map/ppermute | solution.py:28
  31.3 5.0 %collective-permute-start.8 = (bf16[128,512]{1,0:T(8,128)(2,1)S(1)}, bf16[128,512]{1,0:T(8,128)(2,1)S(1)}, u32[]{:S(2)}, u32[]{:S(2)}) collective-permute-start(bf16[128,512]{1,0:T(8,128)(2,1)S(1)} %collective-permute-done.6.refs_1_), channel_id=1, source_target_pairs={{0,8},{1,9},{2,10},{3,11},{4,0},{5,1},{6,2},{7,3},{8,16},{9,17},{1... | collective-permute-start | bytes 393224 | tf_op jit(solution)/shard_map/ppermute | solution.py:28
  33.1 5.0 %collective-permute-start.9 = (bf16[128,512]{1,0:T(8,128)(2,1)S(1)}, bf16[128,512]{1,0:T(8,128)(2,1)S(1)}, u32[]{:S(2)}, u32[]{:S(2)}) collective-permute-start(bf16[128,512]{1,0:T(8,128)(2,1)S(1)} %collective-permute-done.7.refs_2_), channel_id=1, source_target_pairs={{0,4},{1,5},{2,6},{3,7},{4,12},{5,13},{6,14},{7,15},{8,0},{9,1},{1... | collective-permute-start | bytes 393224 | tf_op jit(solution)/shard_map/ppermute | solution.py:28
  36.3 5.6 %collective-permute-start.10 = (bf16[128,512]{1,0:T(8,128)(2,1)S(1)}, bf16[128,512]{1,0:T(8,128)(2,1)S(1)}, u32[]{:S(2)}, u32[]{:S(2)}) collective-permute-start(bf16[128,512]{1,0:T(8,128)(2,1)S(1)} %collective-permute-done.8.refs_3_), channel_id=1, source_target_pairs={{0,8},{1,9},{2,10},{3,11},{4,0},{5,1},{6,2},{7,3},{8,16},{9,17},{1... | collective-permute-start | bytes 393224 | tf_op jit(solution)/shard_map/ppermute | solution.py:28
  38.1 6.3 %collective-permute-start.11 = (bf16[128,512]{1,0:T(8,128)(2,1)S(1)}, bf16[128,512]{1,0:T(8,128)(2,1)S(1)}, u32[]{:S(2)}, u32[]{:S(2)}) collective-permute-start(bf16[128,512]{1,0:T(8,128)(2,1)S(1)} %collective-permute-done.9.refs_4_), channel_id=1, source_target_pairs={{0,4},{1,5},{2,6},{3,7},{4,12},{5,13},{6,14},{7,15},{8,0},{9,1},{1... | collective-permute-start | bytes 393224 | tf_op jit(solution)/shard_map/ppermute | solution.py:28
  41.9 5.0 %collective-permute-start.12 = (bf16[128,512]{1,0:T(8,128)(2,1)S(1)}, bf16[128,512]{1,0:T(8,128)(2,1)S(1)}, u32[]{:S(2)}, u32[]{:S(2)}) collective-permute-start(bf16[128,512]{1,0:T(8,128)(2,1)S(1)} %collective-permute-done.10.refs_5_), channel_id=1, source_target_pairs={{0,8},{1,9},{2,10},{3,11},{4,0},{5,1},{6,2},{7,3},{8,16},{9,17},{1... | collective-permute-start | bytes 393224 | tf_op jit(solution)/shard_map/ppermute | solution.py:28
  47.9 1.9 %collective-permute-start.13 = (bf16[256,128]{1,0:T(8,128)(2,1)S(1)}, bf16[256,128]{1,0:T(8,128)(2,1)S(1)}, u32[]{:S(2)}, u32[]{:S(2)}) collective-permute-start(bf16[256,128]{1,0:T(8,128)(2,1)S(1)} %get-tuple-element.14), channel_id=1, source_target_pairs={{0,1},{1,0},{2,3},{3,2},{4,5},{5,4},{6,7},{7,6},{8,9},{9,8},{10,11... | collective-permute-start | bytes 196616 | tf_op jit(solution)/shard_map/ppermute | solution.py:28
  48.0 4.5 %collective-permute-start.14 = (bf16[256,128]{1,0:T(8,128)(2,1)S(1)}, bf16[256,128]{1,0:T(8,128)(2,1)S(1)}, u32[]{:S(2)}, u32[]{:S(2)}) collective-permute-start(bf16[256,128]{1,0:T(8,128)(2,1)S(1)} %get-tuple-element.15), channel_id=1, source_target_pairs={{0,2},{1,3},{2,0},{3,1},{4,6},{5,7},{6,4},{7,5},{8,10},{9,11},{10,... | collective-permute-start | bytes 196616 | tf_op jit(solution)/shard_map/ppermute | solution.py:28
  49.6 4.1 %collective-permute-start.15 = (bf16[256,128]{1,0:T(8,128)(2,1)S(1)}, bf16[256,128]{1,0:T(8,128)(2,1)S(1)}, u32[]{:S(2)}, u32[]{:S(2)}) collective-permute-start(bf16[256,128]{1,0:T(8,128)(2,1)S(1)} %get-tuple-element.16), channel_id=1, source_target_pairs={{0,3},{1,2},{2,1},{3,0},{4,7},{5,6},{6,5},{7,4},{8,11},{9,10},{10,... | collective-permute-start | bytes 196616 | tf_op jit(solution)/shard_map/ppermute | solution.py:28

commit v3 on v2

--- a/solution.py
+++ b/solution.py
@@ -99,15 +99,20 @@
     blocks, sources = [projection], [list(range(loop_size))]
     forth = back = projection
     forth_from = back_from = sources[0]
-    for _ in range(loop_size // 2 - 1):
+    rounds = loop_size // 2 - 1
+    for step in range(rounds):
+        if step == rounds - 1:
+            opposite = jnp.where(side == 0, forth, back)
+            opposite = move(opposite, sizes, lambda l, s: (behind[behind[l]] if s % 2 else ahead[ahead[l]], s))
+            opposite_from = [forth_from[behind[behind[l]]] for l in range(loop_size)]
         forth = move(forth, sizes, lambda l, s: (ahead[l], s))
         forth_from = [forth_from[behind[l]] for l in range(loop_size)]
         back = move(back, sizes, lambda l, s: (behind[l], s))
         back_from = [back_from[ahead[l]] for l in range(loop_size)]
         blocks += [forth, back]
         sources += [forth_from, back_from]
-    blocks.append(move(forth, sizes, lambda l, s: (ahead[l], s)))
-    sources.append([forth_from[behind[l]] for l in range(loop_size)])
+    blocks.append(opposite)
+    sources.append(opposite_from)
 
     per_chunk = loop_size // seg_size
     held = np.array(sources).T ^ 1

time: 54.5 us -> 53 us (0.972)
  waiting for transfers between devices: 24 us -> 21.5 us
  starting transfers between devices: 23.6 us -> 24.5 us
    ppermute x16, waiting for transfers between devices: 24 us -> 21.5 us  [move(): return lax.ppermute(value, AXES, pairs)]
    ppermute x16, starting transfers between devices: 23.6 us -> 24.5 us  [move(): return lax.ppermute(value, AXES, pairs)]
  transfers between devices with their start and end apart: 16 -> 16, of which waited for: 8 -> 9; matrix products, arithmetic and copies ran while one was open for 5% -> 5% of each run, Pallas kernels for 0% -> 0%
where the time goes in v3:
time: 53 us; the launch traced here: 52.8 us
  starting transfers between devices  24.5 us (46%)
  waiting for transfers between devices  21.5 us (41%)
  matrix products  2.4 us (5%)
  other arithmetic  1.78 us (3%)
  local copies, waits for them, and re-layouts  1.45 us (3%)
  Pallas kernels  1.07 us (2%)
    ppermute x16, starting transfers between devices, move(): return lax.ppermute(value, AXES, pairs)  24.5 us
    ppermute x16, waiting for transfers between devices, move(): return lax.ppermute(value, AXES, pairs)  21.5 us
    dot_general x3, matrix products, product(): lax.dot_general(tile, dosage, (((0,), (1,)), ((), ())), preferred_element...  2.4 us
    pallas_call x1, Pallas kernels, shards(): pl.pallas_call(functools.partial(pair_kernel, loop_size), out_shape=[jax....  1.07 us
  transfers between devices with their start and end apart: 16, of which 9 were waited for; matrix products, arithmetic and copies ran while one was open for 5% of the time, Pallas kernels for 0%

profile of v3, /device:TPU:0, one launch (start us, length us, event | category | flops | bytes accessed | tf_op | source)
XLA Modules:
  0.0 52.8 jit_solution(11914131376986655366)
XLA Ops:
  0.0 0.0 copy-start
  0.0 0.0 copy-start.1
  0.0 0.0 copy-start.2
  0.0 0.7 %copy-done.1 = s32[128]{0:T(128)S(1)} copy-done((s32[128]{0:T(128)S(1)}, s32[128]{0:T(128)}, u32[]{:S(2)}) %copy-start.1) | copy-done | bytes 536
  0.7 0.0 copy-done.2
  0.8 1.0 %bitcast_select_fusion = (bf16[512,128]{1,0:T(8,128)(2,1)S(1)}, bf16[512,128]{1,0:T(8,128)(2,1)S(1)}) fusion(bf16[3,1024,128]{2,1,0:T(8,128)(2,1)} %param.6, s32[]{:T(128)S(6)} %select_n.66, s32[]{:T(128)S(6)} %select_n.64, pred[128]{0:T(512)(128)(4,1)S(1)} %get-tuple-element.23, s32[]{:T(128)S(6)} %select_n.63, pred[128]{0:T(512)(128)(4,1)S(1)} %get-tuple-element.24), kind=kLoop, calls=%fused_computation.13 | loop fusion | flops 131072 | bytes 524556 | tf_op jit(solution)/shard_map/jit(_where)/select_n | solution.py:62
  1.8 0.7 %collective-permute-start.1 = (bf16[512,128]{1,0:T(8,128)(2,1)S(1)}, bf16[512,128]{1,0:T(8,128)(2,1)S(1)}, u32[]{:S(2)}, u32[]{:S(2)}) collective-permute-start(bf16[512,128]{1,0:T(8,128)(2,1)S(1)} %get-tuple-element.17), channel_id=1, source_target_pairs={{0,0},{1,1},{2,2},{3,3},{4,8},{5,9},{6,10},{7,11},{8,4},{9,5},{10,... | collective-permute-start | bytes 393224 | tf_op jit(solution)/shard_map/ppermute | solution.py:28
  2.5 0.0 copy-done
  2.5 1.4 %fusion.9 = f32[128,512]{1,0:T(8,128)S(1)} fusion(bf16[512,1024]{1,0:T(8,128)(2,1)S(1)} %copy-done, bf16[3,1024,128]{2,1,0:T(8,128)(2,1)} %param.6), kind=kOutput, calls=%fused_computation.10 | convolution fusion | flops 134217728 | bytes 1572864 | tf_op jit(solution)/shard_map/dot_general | solution.py:79
  3.9 0.0 collective-permute-done.1
  3.9 0.6 %collective-permute-start.2 = (bf16[512,128]{1,0:T(8,128)(2,1)S(1)}, bf16[512,128]{1,0:T(8,128)(2,1)S(1)}, u32[]{:S(2)}, u32[]{:S(2)}) collective-permute-start(bf16[512,128]{1,0:T(8,128)(2,1)S(1)} %collective-permute-done.1), channel_id=1, source_target_pairs={{0,1},{1,0},{2,3},{3,2},{4,5},{5,4},{6,7},{7,6},{8,9},{9,8},{10,11... | collective-permute-start | bytes 393224 | tf_op jit(solution)/shard_map/ppermute | solution.py:28
  4.5 8.3 %collective-permute-start = (bf16[512,128]{1,0:T(8,128)(2,1)S(1)}, bf16[512,128]{1,0:T(8,128)(2,1)S(1)}, u32[]{:S(2)}, u32[]{:S(2)}) collective-permute-start(bf16[512,128]{1,0:T(8,128)(2,1)S(1)} %get-tuple-element.18), channel_id=1, source_target_pairs={{0,4},{1,5},{2,6},{3,7},{4,0},{5,1},{6,2},{7,3},{8,12},{9,13},{10,... | collective-permute-start | bytes 393224 | tf_op jit(solution)/shard_map/ppermute | solution.py:28
  12.8 0.0 collective-permute-done.2
  12.9 0.5 fusion.2
  13.3 3.6 %collective-permute-done = bf16[512,128]{1,0:T(8,128)(2,1)S(1)} collective-permute-done((bf16[512,128]{1,0:T(8,128)(2,1)S(1)}, bf16[512,128]{1,0:T(8,128)(2,1)S(1)}, u32[]{:S(2)}, u32[]{:S(2)}) %collective-permute-start) | collective-permute-done | bytes 131104 | tf_op jit(solution)/shard_map/ppermute | solution.py:28
  17.0 0.0 collective-permute-start.3
  17.0 1.7 %collective-permute-start.4 = (f32[128,512]{1,0:T(8,128)S(1)}, f32[128,512]{1,0:T(8,128)S(1)}, u32[]{:S(2)}, u32[]{:S(2)}) collective-permute-start(f32[128,512]{1,0:T(8,128)S(1)} %fusion.9), channel_id=1, source_target_pairs={{0,4},{1,5},{2,6},{3,7},{4,0},{5,1},{6,2},{7,3},{8,12},{9,13},{10,... | collective-permute-start | bytes 786440 | tf_op jit(solution)/shard_map/ppermute | solution.py:28
  18.7 2.4 %collective-permute-start.5 = (bf16[128,512]{1,0:T(8,128)(2,1)S(1)}, bf16[128,512]{1,0:T(8,128)(2,1)S(1)}, u32[]{:S(2)}, u32[]{:S(2)}) collective-permute-start(bf16[128,512]{1,0:T(8,128)(2,1)S(1)} %fusion.2), channel_id=1, source_target_pairs={{0,24},{1,25},{2,26},{3,27},{4,12},{5,13},{6,14},{7,15},{8,0},{9,1... | collective-permute-start | bytes 393224 | tf_op jit(solution)/shard_map/ppermute | solution.py:28
  21.1 0.0 collective-permute-done.3
  21.1 4.6 %collective-permute-done.4 = f32[128,512]{1,0:T(8,128)S(1)} collective-permute-done((f32[128,512]{1,0:T(8,128)S(1)}, f32[128,512]{1,0:T(8,128)S(1)}, u32[]{:S(2)}, u32[]{:S(2)}) %collective-permute-start.4) | collective-permute-done | bytes 262176 | tf_op jit(solution)/shard_map/ppermute | solution.py:28
  25.7 0.0 collective-permute-done.5
  25.7 0.5 fusion.1.refs_0_
  26.2 1.8 %collective-permute-start.7 = (bf16[128,512]{1,0:T(8,128)(2,1)S(1)}, bf16[128,512]{1,0:T(8,128)(2,1)S(1)}, u32[]{:S(2)}, u32[]{:S(2)}) collective-permute-start(bf16[128,512]{1,0:T(8,128)(2,1)S(1)} %fusion.1.refs_0_), channel_id=1, source_target_pairs={{0,4},{1,5},{2,6},{3,7},{4,12},{5,13},{6,14},{7,15},{8,0},{9,1},{1... | collective-permute-start | bytes 393224 | tf_op jit(solution)/shard_map/ppermute | solution.py:28
  28.0 0.3 collective-permute-start.6
  28.3 3.1 %collective-permute-done.7.refs_2_ = bf16[128,512]{1,0:T(8,128)(2,1)S(1)} collective-permute-done((bf16[128,512]{1,0:T(8,128)(2,1)S(1)}, bf16[128,512]{1,0:T(8,128)(2,1)S(1)}, u32[]{:S(2)}, u32[]{:S(2)}) %collective-permute-start.7) | collective-permute-done | bytes 131104 | tf_op jit(solution)/shard_map/ppermute | solution.py:28
  31.4 1.7 %collective-permute-start.9 = (bf16[128,512]{1,0:T(8,128)(2,1)S(1)}, bf16[128,512]{1,0:T(8,128)(2,1)S(1)}, u32[]{:S(2)}, u32[]{:S(2)}) collective-permute-start(bf16[128,512]{1,0:T(8,128)(2,1)S(1)} %collective-permute-done.7.refs_2_), channel_id=1, source_target_pairs={{0,4},{1,5},{2,6},{3,7},{4,12},{5,13},{6,14},{7,15},{8,0},{9,1},{1... | collective-permute-start | bytes 393224 | tf_op jit(solution)/shard_map/ppermute | solution.py:28
  33.1 0.0 collective-permute-done.6.refs_1_
  33.1 0.3 collective-permute-start.8
  33.4 2.9 %collective-permute-done.9.refs_4_ = bf16[128,512]{1,0:T(8,128)(2,1)S(1)} collective-permute-done((bf16[128,512]{1,0:T(8,128)(2,1)S(1)}, bf16[128,512]{1,0:T(8,128)(2,1)S(1)}, u32[]{:S(2)}, u32[]{:S(2)}) %collective-permute-start.9) | collective-permute-done | bytes 131104 | tf_op jit(solution)/shard_map/ppermute | solution.py:28
  36.3 1.7 %collective-permute-start.11 = (bf16[128,512]{1,0:T(8,128)(2,1)S(1)}, bf16[128,512]{1,0:T(8,128)(2,1)S(1)}, u32[]{:S(2)}, u32[]{:S(2)}) collective-permute-start(bf16[128,512]{1,0:T(8,128)(2,1)S(1)} %collective-permute-done.9.refs_4_), channel_id=1, source_target_pairs={{0,4},{1,5},{2,6},{3,7},{4,12},{5,13},{6,14},{7,15},{8,0},{9,1},{1... | collective-permute-start | bytes 393224 | tf_op jit(solution)/shard_map/ppermute | solution.py:28
  38.0 0.0 collective-permute-done.8.refs_3_
  38.0 1.6 %collective-permute-start.12 = (bf16[128,512]{1,0:T(8,128)(2,1)S(1)}, bf16[128,512]{1,0:T(8,128)(2,1)S(1)}, u32[]{:S(2)}, u32[]{:S(2)}) collective-permute-start(bf16[128,512]{1,0:T(8,128)(2,1)S(1)} %broadcast_select_fusion), channel_id=1, source_target_pairs={{0,16},{1,13},{2,18},{3,15},{4,8},{5,21},{6,10},{7,23},{8,24},{9,5... | collective-permute-start | bytes 393224 | tf_op jit(solution)/shard_map/ppermute | solution.py:28
  39.6 1.6 %collective-permute-start.10 = (bf16[128,512]{1,0:T(8,128)(2,1)S(1)}, bf16[128,512]{1,0:T(8,128)(2,1)S(1)}, u32[]{:S(2)}, u32[]{:S(2)}) collective-permute-start(bf16[128,512]{1,0:T(8,128)(2,1)S(1)} %collective-permute-done.8.refs_3_), channel_id=1, source_target_pairs={{0,8},{1,9},{2,10},{3,11},{4,0},{5,1},{6,2},{7,3},{8,16},{9,17},{1... | collective-permute-start | bytes 393224 | tf_op jit(solution)/shard_map/ppermute | solution.py:28
  41.2 0.7 %fusion.12.where_ref = s32[17]{0:T(128)S(1)} fusion(s32[32,17]{1,0:T(8,128)} %constant.48.clone, s32[]{:T(128)S(6)} %select_n.59), kind=kLoop, calls=%fused_computation.24 | loop fusion | bytes 140 | tf_op jit(solution)/shard_map/squeeze | solution.py:124
  41.9 1.6 %collective-permute-done.11.refs_6_ = bf16[128,512]{1,0:T(8,128)(2,1)S(1)} collective-permute-done((bf16[128,512]{1,0:T(8,128)(2,1)S(1)}, bf16[128,512]{1,0:T(8,128)(2,1)S(1)}, u32[]{:S(2)}, u32[]{:S(2)}) %collective-permute-start.11) | collective-permute-done | bytes 131104 | tf_op jit(solution)/shard_map/ppermute | solution.py:28
  43.5 1.7 %collective-permute-done.12.refs_7_ = bf16[128,512]{1,0:T(8,128)(2,1)S(1)} collective-permute-done((bf16[128,512]{1,0:T(8,128)(2,1)S(1)}, bf16[128,512]{1,0:T(8,128)(2,1)S(1)}, u32[]{:S(2)}, u32[]{:S(2)}) %collective-permute-start.12) | collective-permute-done | bytes 131104 | tf_op jit(solution)/shard_map/ppermute | solution.py:28
  45.1 0.2 collective-permute-done.10.refs_5_
  45.4 1.1 %pair_sums.1 = (f32[256,128]{1,0:T(8,128)S(1)}, bf16[256,128]{1,0:T(8,128)(2,1)S(1)}, bf16[256,128]{1,0:T(8,128)(2,1)S(1)}, bf16[256,128]{1,0:T(8,128)(2,1)S(1)}) custom-call(s32[17]{0:T(128)S(1)} %fusion.12.where_ref, bf16[128,512]{1,0:T(8,128)(2,1)S(1)} %fusion.1.refs_0_, bf16[128,512]{1,0:T(8,128)(2,1)S(1)} %collective-permute-done.6.refs_1_, ...), custom_call_target="tpu_custom_call" | custom-call | tf_op jit(solution)/shard_map/pair_sums/pallas_call | solution.py:127
  46.5 0.1 collective-permute-start.13
  46.5 1.6 %collective-permute-start.14 = (bf16[256,128]{1,0:T(8,128)(2,1)S(1)}, bf16[256,128]{1,0:T(8,128)(2,1)S(1)}, u32[]{:S(2)}, u32[]{:S(2)}) collective-permute-start(bf16[256,128]{1,0:T(8,128)(2,1)S(1)} %get-tuple-element.15), channel_id=1, source_target_pairs={{0,2},{1,3},{2,0},{3,1},{4,6},{5,7},{6,4},{7,5},{8,10},{9,11},{10,... | collective-permute-start | bytes 196616 | tf_op jit(solution)/shard_map/ppermute | solution.py:28
  48.1 0.3 collective-permute-start.15
  48.4 0.0 collective-permute-done.13
  48.4 2.6 %collective-permute-done.14 = bf16[256,128]{1,0:T(8,128)(2,1)S(1)} collective-permute-done((bf16[256,128]{1,0:T(8,128)(2,1)S(1)}, bf16[256,128]{1,0:T(8,128)(2,1)S(1)}, u32[]{:S(2)}, u32[]{:S(2)}) %collective-permute-start.14) | collective-permute-done | bytes 65568 | tf_op jit(solution)/shard_map/ppermute | solution.py:28
  51.0 1.1 %collective-permute-done.15 = bf16[256,128]{1,0:T(8,128)(2,1)S(1)} collective-permute-done((bf16[256,128]{1,0:T(8,128)(2,1)S(1)}, bf16[256,128]{1,0:T(8,128)(2,1)S(1)}, u32[]{:S(2)}, u32[]{:S(2)}) %collective-permute-start.15) | collective-permute-done | bytes 65568 | tf_op jit(solution)/shard_map/ppermute | solution.py:28
  52.1 0.7 %add_multiply_fusion = f32[256,128]{1,0:T(8,128)} fusion(bf16[256,128]{1,0:T(8,128)(2,1)S(1)} %collective-permute-done.15, bf16[256,128]{1,0:T(8,128)(2,1)S(1)} %collective-permute-done.14, f32[256,128]{1,0:T(8,128)S(1)} %get-tuple-element.13, bf16[256,128]{1,0:T(8,128)(2,1)S(1)} %collective-permute-done.13), kind=kLoop, calls=%fused_computation.15 | loop fusion | flops 229376 | bytes 458752 | tf_op jit(solution)/shard_map/div | solution.py:139
  (4 shorter events, 0.1 us)
Async XLA Ops:
  0.0 2.5 %copy-start = (bf16[512,1024]{1,0:T(8,128)(2,1)S(1)}, bf16[512,1024]{1,0:T(8,128)(2,1)}, u32[]{:S(2)}) copy-start(bf16[512,1024]{1,0:T(8,128)(2,1)} %param.5) | copy-start | bytes 3145732
  0.0 0.7 %copy-start.1 = (s32[128]{0:T(128)S(1)}, s32[128]{0:T(128)}, u32[]{:S(2)}) copy-start(s32[128]{0:T(128)} %param.8) | copy-start | bytes 1540
  0.0 0.8 %copy-start.2 = (s32[128]{0:T(128)S(1)}, s32[128]{0:T(128)}, u32[]{:S(2)}) copy-start(s32[128]{0:T(128)} %param.7) | copy-start | bytes 1540
  1.8 2.1 %collective-permute-start.1 = (bf16[512,128]{1,0:T(8,128)(2,1)S(1)}, bf16[512,128]{1,0:T(8,128)(2,1)S(1)}, u32[]{:S(2)}, u32[]{:S(2)}) collective-permute-start(bf16[512,128]{1,0:T(8,128)(2,1)S(1)} %get-tuple-element.17), channel_id=1, source_target_pairs={{0,0},{1,1},{2,2},{3,3},{4,8},{5,9},{6,10},{7,11},{8,4},{9,5},{10,... | collective-permute-start | bytes 393224 | tf_op jit(solution)/shard_map/ppermute | solution.py:28
  3.9 8.9 %collective-permute-start.2 = (bf16[512,128]{1,0:T(8,128)(2,1)S(1)}, bf16[512,128]{1,0:T(8,128)(2,1)S(1)}, u32[]{:S(2)}, u32[]{:S(2)}) collective-permute-start(bf16[512,128]{1,0:T(8,128)(2,1)S(1)} %collective-permute-done.1), channel_id=1, source_target_pairs={{0,1},{1,0},{2,3},{3,2},{4,5},{5,4},{6,7},{7,6},{8,9},{9,8},{10,11... | collective-permute-start | bytes 393224 | tf_op jit(solution)/shard_map/ppermute | solution.py:28
  4.5 12.5 %collective-permute-start = (bf16[512,128]{1,0:T(8,128)(2,1)S(1)}, bf16[512,128]{1,0:T(8,128)(2,1)S(1)}, u32[]{:S(2)}, u32[]{:S(2)}) collective-permute-start(bf16[512,128]{1,0:T(8,128)(2,1)S(1)} %get-tuple-element.18), channel_id=1, source_target_pairs={{0,4},{1,5},{2,6},{3,7},{4,0},{5,1},{6,2},{7,3},{8,12},{9,13},{10,... | collective-permute-start | bytes 393224 | tf_op jit(solution)/shard_map/ppermute | solution.py:28
  17.0 4.1 %collective-permute-start.3 = (bf16[512,128]{1,0:T(8,128)(2,1)S(1)}, bf16[512,128]{1,0:T(8,128)(2,1)S(1)}, u32[]{:S(2)}, u32[]{:S(2)}) collective-permute-start(bf16[512,128]{1,0:T(8,128)(2,1)S(1)} %collective-permute-done), channel_id=1, source_target_pairs={{0,1},{1,0},{2,3},{3,2},{4,5},{5,4},{6,7},{7,6},{8,9},{9,8},{10,11... | collective-permute-start | bytes 393224 | tf_op jit(solution)/shard_map/ppermute | solution.py:28
  17.0 8.7 %collective-permute-start.4 = (f32[128,512]{1,0:T(8,128)S(1)}, f32[128,512]{1,0:T(8,128)S(1)}, u32[]{:S(2)}, u32[]{:S(2)}) collective-permute-start(f32[128,512]{1,0:T(8,128)S(1)} %fusion.9), channel_id=1, source_target_pairs={{0,4},{1,5},{2,6},{3,7},{4,0},{5,1},{6,2},{7,3},{8,12},{9,13},{10,... | collective-permute-start | bytes 786440 | tf_op jit(solution)/shard_map/ppermute | solution.py:28
  18.7 7.0 %collective-permute-start.5 = (bf16[128,512]{1,0:T(8,128)(2,1)S(1)}, bf16[128,512]{1,0:T(8,128)(2,1)S(1)}, u32[]{:S(2)}, u32[]{:S(2)}) collective-permute-start(bf16[128,512]{1,0:T(8,128)(2,1)S(1)} %fusion.2), channel_id=1, source_target_pairs={{0,24},{1,25},{2,26},{3,27},{4,12},{5,13},{6,14},{7,15},{8,0},{9,1... | collective-permute-start | bytes 393224 | tf_op jit(solution)/shard_map/ppermute | solution.py:28
  26.2 5.2 %collective-permute-start.7 = (bf16[128,512]{1,0:T(8,128)(2,1)S(1)}, bf16[128,512]{1,0:T(8,128)(2,1)S(1)}, u32[]{:S(2)}, u32[]{:S(2)}) collective-permute-start(bf16[128,512]{1,0:T(8,128)(2,1)S(1)} %fusion.1.refs_0_), channel_id=1, source_target_pairs={{0,4},{1,5},{2,6},{3,7},{4,12},{5,13},{6,14},{7,15},{8,0},{9,1},{1... | collective-permute-start | bytes 393224 | tf_op jit(solution)/shard_map/ppermute | solution.py:28
  28.0 5.1 %collective-permute-start.6 = (bf16[128,512]{1,0:T(8,128)(2,1)S(1)}, bf16[128,512]{1,0:T(8,128)(2,1)S(1)}, u32[]{:S(2)}, u32[]{:S(2)}) collective-permute-start(bf16[128,512]{1,0:T(8,128)(2,1)S(1)} %fusion.1.refs_0_), channel_id=1, source_target_pairs={{0,8},{1,9},{2,10},{3,11},{4,0},{5,1},{6,2},{7,3},{8,16},{9,17},{1... | collective-permute-start | bytes 393224 | tf_op jit(solution)/shard_map/ppermute | solution.py:28
  31.4 5.0 %collective-permute-start.9 = (bf16[128,512]{1,0:T(8,128)(2,1)S(1)}, bf16[128,512]{1,0:T(8,128)(2,1)S(1)}, u32[]{:S(2)}, u32[]{:S(2)}) collective-permute-start(bf16[128,512]{1,0:T(8,128)(2,1)S(1)} %collective-permute-done.7.refs_2_), channel_id=1, source_target_pairs={{0,4},{1,5},{2,6},{3,7},{4,12},{5,13},{6,14},{7,15},{8,0},{9,1},{1... | collective-permute-start | bytes 393224 | tf_op jit(solution)/shard_map/ppermute | solution.py:28
  33.1 5.0 %collective-permute-start.8 = (bf16[128,512]{1,0:T(8,128)(2,1)S(1)}, bf16[128,512]{1,0:T(8,128)(2,1)S(1)}, u32[]{:S(2)}, u32[]{:S(2)}) collective-permute-start(bf16[128,512]{1,0:T(8,128)(2,1)S(1)} %collective-permute-done.6.refs_1_), channel_id=1, source_target_pairs={{0,8},{1,9},{2,10},{3,11},{4,0},{5,1},{6,2},{7,3},{8,16},{9,17},{1... | collective-permute-start | bytes 393224 | tf_op jit(solution)/shard_map/ppermute | solution.py:28
  36.3 7.1 %collective-permute-start.11 = (bf16[128,512]{1,0:T(8,128)(2,1)S(1)}, bf16[128,512]{1,0:T(8,128)(2,1)S(1)}, u32[]{:S(2)}, u32[]{:S(2)}) collective-permute-start(bf16[128,512]{1,0:T(8,128)(2,1)S(1)} %collective-permute-done.9.refs_4_), channel_id=1, source_target_pairs={{0,4},{1,5},{2,6},{3,7},{4,12},{5,13},{6,14},{7,15},{8,0},{9,1},{1... | collective-permute-start | bytes 393224 | tf_op jit(solution)/shard_map/ppermute | solution.py:28
  38.0 7.1 %collective-permute-start.12 = (bf16[128,512]{1,0:T(8,128)(2,1)S(1)}, bf16[128,512]{1,0:T(8,128)(2,1)S(1)}, u32[]{:S(2)}, u32[]{:S(2)}) collective-permute-start(bf16[128,512]{1,0:T(8,128)(2,1)S(1)} %broadcast_select_fusion), channel_id=1, source_target_pairs={{0,16},{1,13},{2,18},{3,15},{4,8},{5,21},{6,10},{7,23},{8,24},{9,5... | collective-permute-start | bytes 393224 | tf_op jit(solution)/shard_map/ppermute | solution.py:28
  39.6 5.8 %collective-permute-start.10 = (bf16[128,512]{1,0:T(8,128)(2,1)S(1)}, bf16[128,512]{1,0:T(8,128)(2,1)S(1)}, u32[]{:S(2)}, u32[]{:S(2)}) collective-permute-start(bf16[128,512]{1,0:T(8,128)(2,1)S(1)} %collective-permute-done.8.refs_3_), channel_id=1, source_target_pairs={{0,8},{1,9},{2,10},{3,11},{4,0},{5,1},{6,2},{7,3},{8,16},{9,17},{1... | collective-permute-start | bytes 393224 | tf_op jit(solution)/shard_map/ppermute | solution.py:28
  46.5 1.9 %collective-permute-start.13 = (bf16[256,128]{1,0:T(8,128)(2,1)S(1)}, bf16[256,128]{1,0:T(8,128)(2,1)S(1)}, u32[]{:S(2)}, u32[]{:S(2)}) collective-permute-start(bf16[256,128]{1,0:T(8,128)(2,1)S(1)} %get-tuple-element.14), channel_id=1, source_target_pairs={{0,1},{1,0},{2,3},{3,2},{4,5},{5,4},{6,7},{7,6},{8,9},{9,8},{10,11... | collective-permute-start | bytes 196616 | tf_op jit(solution)/shard_map/ppermute | solution.py:28
  46.5 4.5 %collective-permute-start.14 = (bf16[256,128]{1,0:T(8,128)(2,1)S(1)}, bf16[256,128]{1,0:T(8,128)(2,1)S(1)}, u32[]{:S(2)}, u32[]{:S(2)}) collective-permute-start(bf16[256,128]{1,0:T(8,128)(2,1)S(1)} %get-tuple-element.15), channel_id=1, source_target_pairs={{0,2},{1,3},{2,0},{3,1},{4,6},{5,7},{6,4},{7,5},{8,10},{9,11},{10,... | collective-permute-start | bytes 196616 | tf_op jit(solution)/shard_map/ppermute | solution.py:28
  48.1 4.1 %collective-permute-start.15 = (bf16[256,128]{1,0:T(8,128)(2,1)S(1)}, bf16[256,128]{1,0:T(8,128)(2,1)S(1)}, u32[]{:S(2)}, u32[]{:S(2)}) collective-permute-start(bf16[256,128]{1,0:T(8,128)(2,1)S(1)} %get-tuple-element.16), channel_id=1, source_target_pairs={{0,3},{1,2},{2,1},{3,0},{4,7},{5,6},{6,5},{7,4},{8,11},{9,10},{10,... | collective-permute-start | bytes 196616 | tf_op jit(solution)/shard_map/ppermute | solution.py:28

commit v4 on v3

--- a/solution.py
+++ b/solution.py
@@ -38,9 +38,9 @@
         def _():
             column_ref[...] = block[...]
 
-    column = column_ref[...]
+    column = column_ref[...].T
     for k, block in enumerate(blocks):
-        product = lax.dot_general(block[...], column, (((1,), (1,)), ((), ())), preferred_element_type=jnp.float32)
+        product = jnp.dot(block[...], column, preferred_element_type=jnp.float32)
         row = pl.multiple_of(where_ref[2 * k + 1] * genes, genes)
         sums_ref[where_ref[2 * k], pl.ds(row, genes), :] = product
     own_ref[...] = sums_ref[0]
@@ -56,14 +56,19 @@
     odd, side = place % 2, part % 2
     half = block // 2
 
-    def masked_half(slot, inside):
-        tile = lax.dynamic_slice(weight_tiles, (slot, side * half, 0), (1, half, genes))[0]
-        covered = (slot >= first_tile) & (slot <= last_tile) & inside
-        return jnp.where(covered[None, :], tile, jnp.zeros((), tile.dtype))
+    far_slot = odd * (n_slots - 1)
+    near_slot = n_slots - 1 - far_slot
 
-    far_slot = odd * (n_slots - 1)
-    far_half = masked_half(far_slot, (place > 0) & (place < loop_size - 1))
-    near_half = masked_half(n_slots - 1 - far_slot, True)
+    def half_tile(slot):
+        return lax.dynamic_slice(weight_tiles, (slot, side * half, 0), (1, half, genes))[0]
+
+    def covered(slot):
+        return ((slot >= first_tile) & (slot <= last_tile))[None, :]
+
+    far_half = half_tile(far_slot)
+    far_mask = covered(far_slot) & (place > 0) & (place < loop_size - 1)
+    near_half = jnp.where(covered(near_slot), half_tile(near_slot), jnp.zeros((), weight_tiles.dtype))
+    near_half = jnp.concatenate([near_half, jnp.broadcast_to(far_mask, (16, genes)).astype(near_half.dtype)], axis=0)
 
     def outward(step):
         def target(l, s):
@@ -90,8 +95,10 @@
     home_term = move(home_term, sizes, partner)
     far_term = term(far_half, move(far_half, sizes, sibling))
     near_half, _ = lax.optimization_barrier((near_half, far_term))
+    near_half, far_mask = near_half[:half], near_half[half]
     far_term = move(far_term.astype(jnp.bfloat16), sizes, outward(2))
     near_term = term(near_half, move(near_half, sizes, sibling))
+    far_term = jnp.where(far_mask[:, None] > 0, far_term.astype(jnp.float32), 0.0)
     projection = (near_term + home_term + far_term).astype(jnp.bfloat16)
 
     ahead = [ring_next(loop_size, l) for l in range(loop_size)]

time: 53 us -> 53.9 us (1.017)
  local copies, waits for them, and re-layouts: 1.45 us -> 2.38 us
  starting transfers between devices: 24.5 us -> 25.3 us
  waiting for transfers between devices: 21.5 us -> 20.7 us
    squeeze x0 -> x1, local copies, waits for them, and re-layouts: none -> 1 us  [half_tile(): lax.dynamic_slice(weight_tiles, (slot, side * half, 0), (1, half, genes))[0]]
    ppermute x16, waiting for transfers between devices: 21.5 us -> 20.7 us  [move(): return lax.ppermute(value, AXES, pairs)]
    ppermute x16, starting transfers between devices: 24.5 us -> 25.3 us  [move(): return lax.ppermute(value, AXES, pairs)]
  transfers between devices with their start and end apart: 16 -> 16, of which waited for: 9 -> 9; matrix products, arithmetic and copies ran while one was open for 5% -> 7% of each run, Pallas kernels for 0% -> 0%
where the time goes in v4:
time: 53.9 us; the launch traced here: 53.7 us
  starting transfers between devices  25.3 us (47%)
  waiting for transfers between devices  20.7 us (38%)
  matrix products  2.4 us (4%)
  local copies, waits for them, and re-layouts  2.38 us (4%)
  other arithmetic  1.73 us (3%)
  Pallas kernels  1.07 us (2%)
    ppermute x16, starting transfers between devices, move(): return lax.ppermute(value, AXES, pairs)  25.3 us
    ppermute x16, waiting for transfers between devices, move(): return lax.ppermute(value, AXES, pairs)  20.7 us
    dot_general x3, matrix products, product(): lax.dot_general(tile, dosage, (((0,), (1,)), ((), ())), preferred_element...  2.4 us
  transfers between devices with their start and end apart: 16, of which 9 were waited for; matrix products, arithmetic and copies ran while one was open for 7% of the time, Pallas kernels for 0%

profile of v4, /device:TPU:0, one launch (start us, length us, event | category | flops | bytes accessed | tf_op | source)
XLA Modules:
  0.0 53.7 jit_solution(1492208615353411200)
XLA Ops:
  0.0 0.0 copy-start
  0.0 1.0 %dynamic-slice_bitcast_fusion = bf16[512,128]{1,0:T(8,128)(2,1)S(1)} fusion(bf16[3,1024,128]{2,1,0:T(8,128)(2,1)} %param.6, s32[]{:T(128)S(6)} %select_n.67, s32[]{:T(128)S(6)} %select_n.65), kind=kLoop, calls=%fused_computation.16 | loop fusion | bytes 262152 | tf_op jit(solution)/shard_map/squeeze | solution.py:63
  1.0 0.7 %collective-permute-start.1 = (bf16[512,128]{1,0:T(8,128)(2,1)S(1)}, bf16[512,128]{1,0:T(8,128)(2,1)S(1)}, u32[]{:S(2)}, u32[]{:S(2)}) collective-permute-start(bf16[512,128]{1,0:T(8,128)(2,1)S(1)} %dynamic-slice_bitcast_fusion), channel_id=1, source_target_pairs={{0,0},{1,1},{2,2},{3,3},{4,8},{5,9},{6,10},{7,11},{8,4},{9,5},{10,... | collective-permute-start | bytes 393224 | tf_op jit(solution)/shard_map/ppermute | solution.py:28
  1.7 0.0 copy-done
  1.7 1.4 %fusion.9 = f32[128,512]{1,0:T(8,128)S(1)} fusion(bf16[512,1024]{1,0:T(8,128)(2,1)S(1)} %copy-done, bf16[3,1024,128]{2,1,0:T(8,128)(2,1)} %param.6), kind=kOutput, calls=%fused_computation.10 | convolution fusion | flops 134217728 | bytes 1572864 | tf_op jit(solution)/shard_map/dot_general | solution.py:84
  3.1 5.8 %collective-permute-start.4 = (f32[128,512]{1,0:T(8,128)S(1)}, f32[128,512]{1,0:T(8,128)S(1)}, u32[]{:S(2)}, u32[]{:S(2)}) collective-permute-start(f32[128,512]{1,0:T(8,128)S(1)} %fusion.9), channel_id=1, source_target_pairs={{0,4},{1,5},{2,6},{3,7},{4,0},{5,1},{6,2},{7,3},{8,12},{9,13},{10,... | collective-permute-start | bytes 786440 | tf_op jit(solution)/shard_map/ppermute | solution.py:28
  9.0 0.0 copy-start.1
  9.0 0.0 copy-start.2
  9.0 0.7 %copy-done.1 = s32[128]{0:T(128)S(1)} copy-done((s32[128]{0:T(128)S(1)}, s32[128]{0:T(128)}, u32[]{:S(2)}) %copy-start.1) | copy-done | bytes 536
  9.6 0.0 copy-done.2
  9.6 0.0 collective-permute-done.1
  9.6 0.1 collective-permute-start.2
  9.7 0.9 %bitcast_select_fusion = bf16[512,128]{1,0:T(8,128)(2,1)S(1)} fusion(bf16[3,1024,128]{2,1,0:T(8,128)(2,1)} %param.6, s32[]{:T(128)S(6)} %select_n.64, s32[]{:T(128)S(6)} %select_n.65, pred[128]{0:T(512)(128)(4,1)S(1)} %get-tuple-element.21), kind=kLoop, calls=%fused_computation.14 | loop fusion | flops 65536 | bytes 262280 | tf_op jit(solution)/shard_map/jit(_where)/select_n | solution.py:70
  10.7 2.5 %collective-permute-start = (bf16[528,128]{1,0:T(8,128)(2,1)S(1)}, bf16[528,128]{1,0:T(8,128)(2,1)S(1)}, u32[]{:S(2)}, u32[]{:S(2)}) collective-permute-start(bf16[528,128]{1,0:T(8,128)(2,1)S(1)} %pad_maximum_fusion), channel_id=1, source_target_pairs={{0,4},{1,5},{2,6},{3,7},{4,0},{5,1},{6,2},{7,3},{8,12},{9,13},{10,... | collective-permute-start | bytes 405512 | tf_op jit(solution)/shard_map/ppermute | solution.py:28
  13.2 0.0 collective-permute-done.2
  13.2 0.5 fusion.2
  13.7 4.4 %collective-permute-done = bf16[528,128]{1,0:T(8,128)(2,1)S(1)} collective-permute-done((bf16[528,128]{1,0:T(8,128)(2,1)S(1)}, bf16[528,128]{1,0:T(8,128)(2,1)S(1)}, u32[]{:S(2)}, u32[]{:S(2)}) %collective-permute-start) | collective-permute-done | bytes 135200 | tf_op jit(solution)/shard_map/ppermute | solution.py:28
  18.1 0.1 collective-permute-start.3
  18.2 4.6 %collective-permute-start.5 = (bf16[128,512]{1,0:T(8,128)(2,1)S(1)}, bf16[128,512]{1,0:T(8,128)(2,1)S(1)}, u32[]{:S(2)}, u32[]{:S(2)}) collective-permute-start(bf16[128,512]{1,0:T(8,128)(2,1)S(1)} %fusion.2), channel_id=1, source_target_pairs={{0,24},{1,25},{2,26},{3,27},{4,12},{5,13},{6,14},{7,15},{8,0},{9,1... | collective-permute-start | bytes 393224 | tf_op jit(solution)/shard_map/ppermute | solution.py:28
  22.8 0.0 collective-permute-done.3
  22.8 0.0 collective-permute-done.4
  22.8 3.3 %collective-permute-done.5 = bf16[128,512]{1,0:T(8,128)(2,1)S(1)} collective-permute-done((bf16[128,512]{1,0:T(8,128)(2,1)S(1)}, bf16[128,512]{1,0:T(8,128)(2,1)S(1)}, u32[]{:S(2)}, u32[]{:S(2)}) %collective-permute-start.5) | collective-permute-done | bytes 131104 | tf_op jit(solution)/shard_map/ppermute | solution.py:28
  26.1 0.5 fusion.1.refs_0_
  26.6 2.3 %collective-permute-start.7 = (bf16[128,512]{1,0:T(8,128)(2,1)S(1)}, bf16[128,512]{1,0:T(8,128)(2,1)S(1)}, u32[]{:S(2)}, u32[]{:S(2)}) collective-permute-start(bf16[128,512]{1,0:T(8,128)(2,1)S(1)} %fusion.1.refs_0_), channel_id=1, source_target_pairs={{0,4},{1,5},{2,6},{3,7},{4,12},{5,13},{6,14},{7,15},{8,0},{9,1},{1... | collective-permute-start | bytes 393224 | tf_op jit(solution)/shard_map/ppermute | solution.py:28
  28.9 0.0 collective-permute-start.6
  28.9 2.8 %collective-permute-done.7.refs_2_ = bf16[128,512]{1,0:T(8,128)(2,1)S(1)} collective-permute-done((bf16[128,512]{1,0:T(8,128)(2,1)S(1)}, bf16[128,512]{1,0:T(8,128)(2,1)S(1)}, u32[]{:S(2)}, u32[]{:S(2)}) %collective-permute-start.7) | collective-permute-done | bytes 131104 | tf_op jit(solution)/shard_map/ppermute | solution.py:28
  31.7 2.2 %collective-permute-start.9 = (bf16[128,512]{1,0:T(8,128)(2,1)S(1)}, bf16[128,512]{1,0:T(8,128)(2,1)S(1)}, u32[]{:S(2)}, u32[]{:S(2)}) collective-permute-start(bf16[128,512]{1,0:T(8,128)(2,1)S(1)} %collective-permute-done.7.refs_2_), channel_id=1, source_target_pairs={{0,4},{1,5},{2,6},{3,7},{4,12},{5,13},{6,14},{7,15},{8,0},{9,1},{1... | collective-permute-start | bytes 393224 | tf_op jit(solution)/shard_map/ppermute | solution.py:28
  33.9 0.0 collective-permute-done.6.refs_1_
  33.9 0.0 collective-permute-start.8
  33.9 2.8 %collective-permute-done.9.refs_4_ = bf16[128,512]{1,0:T(8,128)(2,1)S(1)} collective-permute-done((bf16[128,512]{1,0:T(8,128)(2,1)S(1)}, bf16[128,512]{1,0:T(8,128)(2,1)S(1)}, u32[]{:S(2)}, u32[]{:S(2)}) %collective-permute-start.9) | collective-permute-done | bytes 131104 | tf_op jit(solution)/shard_map/ppermute | solution.py:28
  36.6 2.2 %collective-permute-start.11 = (bf16[128,512]{1,0:T(8,128)(2,1)S(1)}, bf16[128,512]{1,0:T(8,128)(2,1)S(1)}, u32[]{:S(2)}, u32[]{:S(2)}) collective-permute-start(bf16[128,512]{1,0:T(8,128)(2,1)S(1)} %collective-permute-done.9.refs_4_), channel_id=1, source_target_pairs={{0,4},{1,5},{2,6},{3,7},{4,12},{5,13},{6,14},{7,15},{8,0},{9,1},{1... | collective-permute-start | bytes 393224 | tf_op jit(solution)/shard_map/ppermute | solution.py:28
  38.8 0.0 collective-permute-done.8.refs_3_
  38.9 1.0 %collective-permute-start.12 = (bf16[128,512]{1,0:T(8,128)(2,1)S(1)}, bf16[128,512]{1,0:T(8,128)(2,1)S(1)}, u32[]{:S(2)}, u32[]{:S(2)}) collective-permute-start(bf16[128,512]{1,0:T(8,128)(2,1)S(1)} %broadcast_select_fusion), channel_id=1, source_target_pairs={{0,16},{1,13},{2,18},{3,15},{4,8},{5,21},{6,10},{7,23},{8,24},{9,5... | collective-permute-start | bytes 393224 | tf_op jit(solution)/shard_map/ppermute | solution.py:28
  39.8 2.0 %collective-permute-start.10 = (bf16[128,512]{1,0:T(8,128)(2,1)S(1)}, bf16[128,512]{1,0:T(8,128)(2,1)S(1)}, u32[]{:S(2)}, u32[]{:S(2)}) collective-permute-start(bf16[128,512]{1,0:T(8,128)(2,1)S(1)} %collective-permute-done.8.refs_3_), channel_id=1, source_target_pairs={{0,8},{1,9},{2,10},{3,11},{4,0},{5,1},{6,2},{7,3},{8,16},{9,17},{1... | collective-permute-start | bytes 393224 | tf_op jit(solution)/shard_map/ppermute | solution.py:28
  41.9 0.7 %fusion.12.where_ref = s32[17]{0:T(128)S(1)} fusion(s32[32,17]{1,0:T(8,128)} %constant.51.clone, s32[]{:T(128)S(6)} %select_n.60), kind=kLoop, calls=%fused_computation.26 | loop fusion | bytes 140 | tf_op jit(solution)/shard_map/squeeze | solution.py:131
  42.5 0.4 collective-permute-done.11.refs_6_
  43.0 2.2 %collective-permute-done.12.refs_7_ = bf16[128,512]{1,0:T(8,128)(2,1)S(1)} collective-permute-done((bf16[128,512]{1,0:T(8,128)(2,1)S(1)}, bf16[128,512]{1,0:T(8,128)(2,1)S(1)}, u32[]{:S(2)}, u32[]{:S(2)}) %collective-permute-start.12) | collective-permute-done | bytes 131104 | tf_op jit(solution)/shard_map/ppermute | solution.py:28
  45.2 1.0 %collective-permute-done.10.refs_5_ = bf16[128,512]{1,0:T(8,128)(2,1)S(1)} collective-permute-done((bf16[128,512]{1,0:T(8,128)(2,1)S(1)}, bf16[128,512]{1,0:T(8,128)(2,1)S(1)}, u32[]{:S(2)}, u32[]{:S(2)}) %collective-permute-start.10) | collective-permute-done | bytes 131104 | tf_op jit(solution)/shard_map/ppermute | solution.py:28
  46.2 1.1 %pair_sums.1 = (f32[256,128]{1,0:T(8,128)S(1)}, bf16[256,128]{1,0:T(8,128)(2,1)S(1)}, bf16[256,128]{1,0:T(8,128)(2,1)S(1)}, bf16[256,128]{1,0:T(8,128)(2,1)S(1)}) custom-call(s32[17]{0:T(128)S(1)} %fusion.12.where_ref, bf16[128,512]{1,0:T(8,128)(2,1)S(1)} %fusion.1.refs_0_, bf16[128,512]{1,0:T(8,128)(2,1)S(1)} %collective-permute-done.6.refs_1_, ...), custom_call_target="tpu_custom_call" | custom-call | tf_op jit(solution)/shard_map/pair_sums/pallas_call | solution.py:134
  47.3 0.1 collective-permute-start.13
  47.4 1.6 %collective-permute-start.14 = (bf16[256,128]{1,0:T(8,128)(2,1)S(1)}, bf16[256,128]{1,0:T(8,128)(2,1)S(1)}, u32[]{:S(2)}, u32[]{:S(2)}) collective-permute-start(bf16[256,128]{1,0:T(8,128)(2,1)S(1)} %get-tuple-element.15), channel_id=1, source_target_pairs={{0,2},{1,3},{2,0},{3,1},{4,6},{5,7},{6,4},{7,5},{8,10},{9,11},{10,... | collective-permute-start | bytes 196616 | tf_op jit(solution)/shard_map/ppermute | solution.py:28
  48.9 0.3 collective-permute-start.15
  49.2 0.0 collective-permute-done.13
  49.2 2.6 %collective-permute-done.14 = bf16[256,128]{1,0:T(8,128)(2,1)S(1)} collective-permute-done((bf16[256,128]{1,0:T(8,128)(2,1)S(1)}, bf16[256,128]{1,0:T(8,128)(2,1)S(1)}, u32[]{:S(2)}, u32[]{:S(2)}) %collective-permute-start.14) | collective-permute-done | bytes 65568 | tf_op jit(solution)/shard_map/ppermute | solution.py:28
  51.9 1.1 %collective-permute-done.15 = bf16[256,128]{1,0:T(8,128)(2,1)S(1)} collective-permute-done((bf16[256,128]{1,0:T(8,128)(2,1)S(1)}, bf16[256,128]{1,0:T(8,128)(2,1)S(1)}, u32[]{:S(2)}, u32[]{:S(2)}) %collective-permute-start.15) | collective-permute-done | bytes 65568 | tf_op jit(solution)/shard_map/ppermute | solution.py:28
  53.0 0.7 %add_multiply_fusion = f32[256,128]{1,0:T(8,128)} fusion(bf16[256,128]{1,0:T(8,128)(2,1)S(1)} %collective-permute-done.15, bf16[256,128]{1,0:T(8,128)(2,1)S(1)} %collective-permute-done.14, f32[256,128]{1,0:T(8,128)S(1)} %get-tuple-element.13, bf16[256,128]{1,0:T(8,128)(2,1)S(1)} %collective-permute-done.13), kind=kLoop, calls=%fused_computation.15 | loop fusion | flops 229376 | bytes 458752 | tf_op jit(solution)/shard_map/div | solution.py:146
  (8 shorter events, 0.1 us)
Async XLA Ops:
  0.0 1.7 %copy-start = (bf16[512,1024]{1,0:T(8,128)(2,1)S(1)}, bf16[512,1024]{1,0:T(8,128)(2,1)}, u32[]{:S(2)}) copy-start(bf16[512,1024]{1,0:T(8,128)(2,1)} %param.5) | copy-start | bytes 3145732
  1.0 8.6 %collective-permute-start.1 = (bf16[512,128]{1,0:T(8,128)(2,1)S(1)}, bf16[512,128]{1,0:T(8,128)(2,1)S(1)}, u32[]{:S(2)}, u32[]{:S(2)}) collective-permute-start(bf16[512,128]{1,0:T(8,128)(2,1)S(1)} %dynamic-slice_bitcast_fusion), channel_id=1, source_target_pairs={{0,0},{1,1},{2,2},{3,3},{4,8},{5,9},{6,10},{7,11},{8,4},{9,5},{10,... | collective-permute-start | bytes 393224 | tf_op jit(solution)/shard_map/ppermute | solution.py:28
  3.1 19.7 %collective-permute-start.4 = (f32[128,512]{1,0:T(8,128)S(1)}, f32[128,512]{1,0:T(8,128)S(1)}, u32[]{:S(2)}, u32[]{:S(2)}) collective-permute-start(f32[128,512]{1,0:T(8,128)S(1)} %fusion.9), channel_id=1, source_target_pairs={{0,4},{1,5},{2,6},{3,7},{4,0},{5,1},{6,2},{7,3},{8,12},{9,13},{10,... | collective-permute-start | bytes 786440 | tf_op jit(solution)/shard_map/ppermute | solution.py:28
  9.0 0.7 %copy-start.1 = (s32[128]{0:T(128)S(1)}, s32[128]{0:T(128)}, u32[]{:S(2)}) copy-start(s32[128]{0:T(128)} %param.8) | copy-start | bytes 1540
  9.0 0.7 %copy-start.2 = (s32[128]{0:T(128)S(1)}, s32[128]{0:T(128)}, u32[]{:S(2)}) copy-start(s32[128]{0:T(128)} %param.7) | copy-start | bytes 1540
  9.6 3.5 %collective-permute-start.2 = (bf16[512,128]{1,0:T(8,128)(2,1)S(1)}, bf16[512,128]{1,0:T(8,128)(2,1)S(1)}, u32[]{:S(2)}, u32[]{:S(2)}) collective-permute-start(bf16[512,128]{1,0:T(8,128)(2,1)S(1)} %collective-permute-done.1), channel_id=1, source_target_pairs={{0,1},{1,0},{2,3},{3,2},{4,5},{5,4},{6,7},{7,6},{8,9},{9,8},{10,11... | collective-permute-start | bytes 393224 | tf_op jit(solution)/shard_map/ppermute | solution.py:28
  10.7 7.4 %collective-permute-start = (bf16[528,128]{1,0:T(8,128)(2,1)S(1)}, bf16[528,128]{1,0:T(8,128)(2,1)S(1)}, u32[]{:S(2)}, u32[]{:S(2)}) collective-permute-start(bf16[528,128]{1,0:T(8,128)(2,1)S(1)} %pad_maximum_fusion), channel_id=1, source_target_pairs={{0,4},{1,5},{2,6},{3,7},{4,0},{5,1},{6,2},{7,3},{8,12},{9,13},{10,... | collective-permute-start | bytes 405512 | tf_op jit(solution)/shard_map/ppermute | solution.py:28
  18.1 4.7 %collective-permute-start.3 = (bf16[512,128]{1,0:T(8,128)(2,1)S(1)}, bf16[512,128]{1,0:T(8,128)(2,1)S(1)}, u32[]{:S(2)}, u32[]{:S(2)}) collective-permute-start(bf16[512,128]{1,0:T(8,128)(2,1)S(1)} %slice.10), channel_id=1, source_target_pairs={{0,1},{1,0},{2,3},{3,2},{4,5},{5,4},{6,7},{7,6},{8,9},{9,8},{10,11... | collective-permute-start | bytes 393224 | tf_op jit(solution)/shard_map/ppermute | solution.py:28
  18.2 8.0 %collective-permute-start.5 = (bf16[128,512]{1,0:T(8,128)(2,1)S(1)}, bf16[128,512]{1,0:T(8,128)(2,1)S(1)}, u32[]{:S(2)}, u32[]{:S(2)}) collective-permute-start(bf16[128,512]{1,0:T(8,128)(2,1)S(1)} %fusion.2), channel_id=1, source_target_pairs={{0,24},{1,25},{2,26},{3,27},{4,12},{5,13},{6,14},{7,15},{8,0},{9,1... | collective-permute-start | bytes 393224 | tf_op jit(solution)/shard_map/ppermute | solution.py:28
  26.6 5.0 %collective-permute-start.7 = (bf16[128,512]{1,0:T(8,128)(2,1)S(1)}, bf16[128,512]{1,0:T(8,128)(2,1)S(1)}, u32[]{:S(2)}, u32[]{:S(2)}) collective-permute-start(bf16[128,512]{1,0:T(8,128)(2,1)S(1)} %fusion.1.refs_0_), channel_id=1, source_target_pairs={{0,4},{1,5},{2,6},{3,7},{4,12},{5,13},{6,14},{7,15},{8,0},{9,1},{1... | collective-permute-start | bytes 393224 | tf_op jit(solution)/shard_map/ppermute | solution.py:28
  28.9 5.0 %collective-permute-start.6 = (bf16[128,512]{1,0:T(8,128)(2,1)S(1)}, bf16[128,512]{1,0:T(8,128)(2,1)S(1)}, u32[]{:S(2)}, u32[]{:S(2)}) collective-permute-start(bf16[128,512]{1,0:T(8,128)(2,1)S(1)} %fusion.1.refs_0_), channel_id=1, source_target_pairs={{0,8},{1,9},{2,10},{3,11},{4,0},{5,1},{6,2},{7,3},{8,16},{9,17},{1... | collective-permute-start | bytes 393224 | tf_op jit(solution)/shard_map/ppermute | solution.py:28
  31.7 5.0 %collective-permute-start.9 = (bf16[128,512]{1,0:T(8,128)(2,1)S(1)}, bf16[128,512]{1,0:T(8,128)(2,1)S(1)}, u32[]{:S(2)}, u32[]{:S(2)}) collective-permute-start(bf16[128,512]{1,0:T(8,128)(2,1)S(1)} %collective-permute-done.7.refs_2_), channel_id=1, source_target_pairs={{0,4},{1,5},{2,6},{3,7},{4,12},{5,13},{6,14},{7,15},{8,0},{9,1},{1... | collective-permute-start | bytes 393224 | tf_op jit(solution)/shard_map/ppermute | solution.py:28
  33.9 5.0 %collective-permute-start.8 = (bf16[128,512]{1,0:T(8,128)(2,1)S(1)}, bf16[128,512]{1,0:T(8,128)(2,1)S(1)}, u32[]{:S(2)}, u32[]{:S(2)}) collective-permute-start(bf16[128,512]{1,0:T(8,128)(2,1)S(1)} %collective-permute-done.6.refs_1_), channel_id=1, source_target_pairs={{0,8},{1,9},{2,10},{3,11},{4,0},{5,1},{6,2},{7,3},{8,16},{9,17},{1... | collective-permute-start | bytes 393224 | tf_op jit(solution)/shard_map/ppermute | solution.py:28
  36.6 6.3 %collective-permute-start.11 = (bf16[128,512]{1,0:T(8,128)(2,1)S(1)}, bf16[128,512]{1,0:T(8,128)(2,1)S(1)}, u32[]{:S(2)}, u32[]{:S(2)}) collective-permute-start(bf16[128,512]{1,0:T(8,128)(2,1)S(1)} %collective-permute-done.9.refs_4_), channel_id=1, source_target_pairs={{0,4},{1,5},{2,6},{3,7},{4,12},{5,13},{6,14},{7,15},{8,0},{9,1},{1... | collective-permute-start | bytes 393224 | tf_op jit(solution)/shard_map/ppermute | solution.py:28
  38.9 6.3 %collective-permute-start.12 = (bf16[128,512]{1,0:T(8,128)(2,1)S(1)}, bf16[128,512]{1,0:T(8,128)(2,1)S(1)}, u32[]{:S(2)}, u32[]{:S(2)}) collective-permute-start(bf16[128,512]{1,0:T(8,128)(2,1)S(1)} %broadcast_select_fusion), channel_id=1, source_target_pairs={{0,16},{1,13},{2,18},{3,15},{4,8},{5,21},{6,10},{7,23},{8,24},{9,5... | collective-permute-start | bytes 393224 | tf_op jit(solution)/shard_map/ppermute | solution.py:28
  39.8 6.4 %collective-permute-start.10 = (bf16[128,512]{1,0:T(8,128)(2,1)S(1)}, bf16[128,512]{1,0:T(8,128)(2,1)S(1)}, u32[]{:S(2)}, u32[]{:S(2)}) collective-permute-start(bf16[128,512]{1,0:T(8,128)(2,1)S(1)} %collective-permute-done.8.refs_3_), channel_id=1, source_target_pairs={{0,8},{1,9},{2,10},{3,11},{4,0},{5,1},{6,2},{7,3},{8,16},{9,17},{1... | collective-permute-start | bytes 393224 | tf_op jit(solution)/shard_map/ppermute | solution.py:28
  47.3 1.9 %collective-permute-start.13 = (bf16[256,128]{1,0:T(8,128)(2,1)S(1)}, bf16[256,128]{1,0:T(8,128)(2,1)S(1)}, u32[]{:S(2)}, u32[]{:S(2)}) collective-permute-start(bf16[256,128]{1,0:T(8,128)(2,1)S(1)} %get-tuple-element.14), channel_id=1, source_target_pairs={{0,1},{1,0},{2,3},{3,2},{4,5},{5,4},{6,7},{7,6},{8,9},{9,8},{10,11... | collective-permute-start | bytes 196616 | tf_op jit(solution)/shard_map/ppermute | solution.py:28
  47.4 4.5 %collective-permute-start.14 = (bf16[256,128]{1,0:T(8,128)(2,1)S(1)}, bf16[256,128]{1,0:T(8,128)(2,1)S(1)}, u32[]{:S(2)}, u32[]{:S(2)}) collective-permute-start(bf16[256,128]{1,0:T(8,128)(2,1)S(1)} %get-tuple-element.15), channel_id=1, source_target_pairs={{0,2},{1,3},{2,0},{3,1},{4,6},{5,7},{6,4},{7,5},{8,10},{9,11},{10,... | collective-permute-start | bytes 196616 | tf_op jit(solution)/shard_map/ppermute | solution.py:28
  48.9 4.1 %collective-permute-start.15 = (bf16[256,128]{1,0:T(8,128)(2,1)S(1)}, bf16[256,128]{1,0:T(8,128)(2,1)S(1)}, u32[]{:S(2)}, u32[]{:S(2)}) collective-permute-start(bf16[256,128]{1,0:T(8,128)(2,1)S(1)} %get-tuple-element.16), channel_id=1, source_target_pairs={{0,3},{1,2},{2,1},{3,0},{4,7},{5,6},{6,5},{7,4},{8,11},{9,10},{10,... | collective-permute-start | bytes 196616 | tf_op jit(solution)/shard_map/ppermute | solution.py:28

commit v5 on v4

--- a/solution.py
+++ b/solution.py
@@ -1,4 +1,5 @@
 import functools
+import math
 
 import jax
 import jax.numpy as jnp
@@ -10,6 +11,7 @@
 
 
 AXES = ("loop", "seg")
+DOSAGE_MAX, WEIGHT_MAX = 3.0, 0.109375
 
 
 def ring_next(loop_size, place):
@@ -73,12 +75,17 @@
     def outward(step):
         def target(l, s):
             to = l + step if l % 2 else l - step
-            return (to if 0 <= to < loop_size else (l if step == 1 else (l - 2) % loop_size if l % 2 == 0 else (l + 2) % loop_size), s)
+            return (to if 0 <= to < loop_size else (l if step == 1 else l ^ 1), s)
 
         return target
 
     partner = lambda l, s: (l ^ 1, s)
     sibling = lambda l, s: (l, s ^ 1)
+
+    scale = 2.0 ** math.floor(math.log2(float(jnp.finfo(jnp.float16).max) / (block * DOSAGE_MAX * WEIGHT_MAX)))
+
+    def packed(term):
+        return (term * scale).astype(jnp.float16)
 
     def product(tile):
         return lax.dot_general(tile, dosage, (((0,), (1,)), ((), ())), preferred_element_type=jnp.float32)
@@ -92,14 +99,14 @@
     near_half = move(near_half, sizes, partner)
     home_term = product(weight_tiles[n_slots // 2])
     far_half, _ = lax.optimization_barrier((far_half, home_term))
-    home_term = move(home_term, sizes, partner)
+    home_term = move(packed(home_term), sizes, partner)
     far_term = term(far_half, move(far_half, sizes, sibling))
     near_half, _ = lax.optimization_barrier((near_half, far_term))
     near_half, far_mask = near_half[:half], near_half[half]
-    far_term = move(far_term.astype(jnp.bfloat16), sizes, outward(2))
+    far_term = move(packed(far_term), sizes, outward(2))
     near_term = term(near_half, move(near_half, sizes, sibling))
     far_term = jnp.where(far_mask[:, None] > 0, far_term.astype(jnp.float32), 0.0)
-    projection = (near_term + home_term + far_term).astype(jnp.bfloat16)
+    projection = (near_term + (home_term.astype(jnp.float32) + far_term) * (1.0 / scale)).astype(jnp.bfloat16)
 
     ahead = [ring_next(loop_size, l) for l in range(loop_size)]
     behind = [ahead.index(l) for l in range(loop_size)]

time: 53.9 us -> 51.1 us (0.948)
  starting transfers between devices: 25.3 us -> 21.7 us
  waiting for transfers between devices: 20.7 us -> 21.4 us
    ppermute x16, starting transfers between devices: 25.3 us -> 21.7 us  [move(): return lax.ppermute(value, AXES, pairs)]
    ppermute x16, waiting for transfers between devices: 20.7 us -> 21.4 us  [move(): return lax.ppermute(value, AXES, pairs)]
  transfers between devices with their start and end apart: 16 -> 16, of which waited for: 9 -> 10; matrix products, arithmetic and copies ran while one was open for 7% -> 7% of each run, Pallas kernels for 0% -> 0%
where the time goes in v5:
time: 51.1 us; the launch traced here: 50.8 us
  starting transfers between devices  21.7 us (42%)
  waiting for transfers between devices  21.4 us (42%)
  matrix products  2.4 us (5%)
  local copies, waits for them, and re-layouts  2.36 us (5%)
  other arithmetic  1.72 us (3%)
  Pallas kernels  1.07 us (2%)
    ppermute x16, starting transfers between devices, move(): return lax.ppermute(value, AXES, pairs)  21.7 us
    ppermute x16, waiting for transfers between devices, move(): return lax.ppermute(value, AXES, pairs)  21.4 us
    dot_general x3, matrix products, product(): lax.dot_general(tile, dosage, (((0,), (1,)), ((), ())), preferred_element...  2.4 us
    pallas_call x1, Pallas kernels, shards(): pl.pallas_call(functools.partial(pair_kernel, loop_size), out_shape=[jax....  1.07 us
  transfers between devices with their start and end apart: 16, of which 10 were waited for; matrix products, arithmetic and copies ran while one was open for 7% of the time, Pallas kernels for 0%

profile of v5, /device:TPU:0, one launch (start us, length us, event | category | flops | bytes accessed | tf_op | source)
XLA Modules:
  0.0 50.8 jit_solution(6145966344932321844)
XLA Ops:
  0.0 0.0 copy-start
  0.0 1.0 %dynamic-slice_bitcast_fusion = bf16[512,128]{1,0:T(8,128)(2,1)S(1)} fusion(bf16[3,1024,128]{2,1,0:T(8,128)(2,1)} %param.6, s32[]{:T(128)S(6)} %select_n.67, s32[]{:T(128)S(6)} %select_n.65), kind=kLoop, calls=%fused_computation.17 | loop fusion | bytes 262152 | tf_op jit(solution)/shard_map/squeeze | solution.py:65
  1.0 0.7 %collective-permute-start.1 = (bf16[512,128]{1,0:T(8,128)(2,1)S(1)}, bf16[512,128]{1,0:T(8,128)(2,1)S(1)}, u32[]{:S(2)}, u32[]{:S(2)}) collective-permute-start(bf16[512,128]{1,0:T(8,128)(2,1)S(1)} %dynamic-slice_bitcast_fusion), channel_id=1, source_target_pairs={{0,0},{1,1},{2,2},{3,3},{4,8},{5,9},{6,10},{7,11},{8,4},{9,5},{10,... | collective-permute-start | bytes 393224 | tf_op jit(solution)/shard_map/ppermute | solution.py:30
  1.7 0.0 copy-done
  1.7 1.4 %multiply_convert_fusion.1 = f16[128,512]{1,0:T(8,128)(2,1)S(1)} fusion(bf16[512,1024]{1,0:T(8,128)(2,1)S(1)} %copy-done, bf16[3,1024,128]{2,1,0:T(8,128)(2,1)} %param.6), kind=kOutput, calls=%fused_computation.12 | convolution fusion | flops 134348800 | bytes 1441792 | tf_op jit(solution)/shard_map/dot_general | solution.py:91
  3.2 0.0 copy-start.1
  3.2 0.0 copy-start.2
  3.2 0.6 %copy-done.1 = s32[128]{0:T(128)S(1)} copy-done((s32[128]{0:T(128)S(1)}, s32[128]{0:T(128)}, u32[]{:S(2)}) %copy-start.1) | copy-done | bytes 536
  3.8 0.0 copy-done.2
  3.8 0.0 collective-permute-done.1
  3.8 0.6 %collective-permute-start.2 = (bf16[512,128]{1,0:T(8,128)(2,1)S(1)}, bf16[512,128]{1,0:T(8,128)(2,1)S(1)}, u32[]{:S(2)}, u32[]{:S(2)}) collective-permute-start(bf16[512,128]{1,0:T(8,128)(2,1)S(1)} %collective-permute-done.1), channel_id=1, source_target_pairs={{0,1},{1,0},{2,3},{3,2},{4,5},{5,4},{6,7},{7,6},{8,9},{9,8},{10,11... | collective-permute-start | bytes 393224 | tf_op jit(solution)/shard_map/ppermute | solution.py:30
  4.4 0.9 %bitcast_select_fusion = bf16[512,128]{1,0:T(8,128)(2,1)S(1)} fusion(bf16[3,1024,128]{2,1,0:T(8,128)(2,1)} %param.6, s32[]{:T(128)S(6)} %select_n.64, s32[]{:T(128)S(6)} %select_n.65, pred[128]{0:T(512)(128)(4,1)S(1)} %get-tuple-element.21), kind=kLoop, calls=%fused_computation.15 | loop fusion | flops 65536 | bytes 262280 | tf_op jit(solution)/shard_map/jit(_where)/select_n | solution.py:72
  5.4 7.7 %collective-permute-start = (bf16[528,128]{1,0:T(8,128)(2,1)S(1)}, bf16[528,128]{1,0:T(8,128)(2,1)S(1)}, u32[]{:S(2)}, u32[]{:S(2)}) collective-permute-start(bf16[528,128]{1,0:T(8,128)(2,1)S(1)} %pad_maximum_fusion), channel_id=1, source_target_pairs={{0,4},{1,5},{2,6},{3,7},{4,0},{5,1},{6,2},{7,3},{8,12},{9,13},{10,... | collective-permute-start | bytes 405512 | tf_op jit(solution)/shard_map/ppermute | solution.py:30
  13.1 0.1 collective-permute-start.4
  13.1 0.0 collective-permute-done.2
  13.2 0.5 multiply_convert_fusion
  13.7 3.8 %collective-permute-done = bf16[528,128]{1,0:T(8,128)(2,1)S(1)} collective-permute-done((bf16[528,128]{1,0:T(8,128)(2,1)S(1)}, bf16[528,128]{1,0:T(8,128)(2,1)S(1)}, u32[]{:S(2)}, u32[]{:S(2)}) %collective-permute-start) | collective-permute-done | bytes 135200 | tf_op jit(solution)/shard_map/ppermute | solution.py:30
  17.5 0.1 collective-permute-start.3
  17.6 2.1 %collective-permute-start.5 = (f16[128,512]{1,0:T(8,128)(2,1)S(1)}, f16[128,512]{1,0:T(8,128)(2,1)S(1)}, u32[]{:S(2)}, u32[]{:S(2)}) collective-permute-start(f16[128,512]{1,0:T(8,128)(2,1)S(1)} %multiply_convert_fusion), channel_id=1, source_target_pairs={{0,4},{1,5},{2,6},{3,7},{4,12},{5,13},{6,14},{7,15},{8,0},{9,1},{1... | collective-permute-start | bytes 393224 | tf_op jit(solution)/shard_map/ppermute | solution.py:30
  19.7 0.0 collective-permute-done.3
  19.7 0.4 collective-permute-done.4
  20.1 3.7 %collective-permute-done.5 = f16[128,512]{1,0:T(8,128)(2,1)S(1)} collective-permute-done((f16[128,512]{1,0:T(8,128)(2,1)S(1)}, f16[128,512]{1,0:T(8,128)(2,1)S(1)}, u32[]{:S(2)}, u32[]{:S(2)}) %collective-permute-start.5) | collective-permute-done | bytes 131104 | tf_op jit(solution)/shard_map/ppermute | solution.py:30
  23.8 0.5 fusion.refs_0_
  24.3 1.7 %collective-permute-start.7 = (bf16[128,512]{1,0:T(8,128)(2,1)S(1)}, bf16[128,512]{1,0:T(8,128)(2,1)S(1)}, u32[]{:S(2)}, u32[]{:S(2)}) collective-permute-start(bf16[128,512]{1,0:T(8,128)(2,1)S(1)} %fusion.refs_0_), channel_id=1, source_target_pairs={{0,4},{1,5},{2,6},{3,7},{4,12},{5,13},{6,14},{7,15},{8,0},{9,1},{1... | collective-permute-start | bytes 393224 | tf_op jit(solution)/shard_map/ppermute | solution.py:30
  26.1 0.3 collective-permute-start.6
  26.4 3.2 %collective-permute-done.7.refs_2_ = bf16[128,512]{1,0:T(8,128)(2,1)S(1)} collective-permute-done((bf16[128,512]{1,0:T(8,128)(2,1)S(1)}, bf16[128,512]{1,0:T(8,128)(2,1)S(1)}, u32[]{:S(2)}, u32[]{:S(2)}) %collective-permute-start.7) | collective-permute-done | bytes 131104 | tf_op jit(solution)/shard_map/ppermute | solution.py:30
  29.6 1.4 %collective-permute-start.9 = (bf16[128,512]{1,0:T(8,128)(2,1)S(1)}, bf16[128,512]{1,0:T(8,128)(2,1)S(1)}, u32[]{:S(2)}, u32[]{:S(2)}) collective-permute-start(bf16[128,512]{1,0:T(8,128)(2,1)S(1)} %collective-permute-done.7.refs_2_), channel_id=1, source_target_pairs={{0,4},{1,5},{2,6},{3,7},{4,12},{5,13},{6,14},{7,15},{8,0},{9,1},{1... | collective-permute-start | bytes 393224 | tf_op jit(solution)/shard_map/ppermute | solution.py:30
  31.1 0.0 collective-permute-done.6.refs_1_
  31.1 0.6 %collective-permute-start.8 = (bf16[128,512]{1,0:T(8,128)(2,1)S(1)}, bf16[128,512]{1,0:T(8,128)(2,1)S(1)}, u32[]{:S(2)}, u32[]{:S(2)}) collective-permute-start(bf16[128,512]{1,0:T(8,128)(2,1)S(1)} %collective-permute-done.6.refs_1_), channel_id=1, source_target_pairs={{0,8},{1,9},{2,10},{3,11},{4,0},{5,1},{6,2},{7,3},{8,16},{9,17},{1... | collective-permute-start | bytes 393224 | tf_op jit(solution)/shard_map/ppermute | solution.py:30
  31.7 2.9 %collective-permute-done.9.refs_4_ = bf16[128,512]{1,0:T(8,128)(2,1)S(1)} collective-permute-done((bf16[128,512]{1,0:T(8,128)(2,1)S(1)}, bf16[128,512]{1,0:T(8,128)(2,1)S(1)}, u32[]{:S(2)}, u32[]{:S(2)}) %collective-permute-start.9) | collective-permute-done | bytes 131104 | tf_op jit(solution)/shard_map/ppermute | solution.py:30
  34.6 1.4 %collective-permute-start.11 = (bf16[128,512]{1,0:T(8,128)(2,1)S(1)}, bf16[128,512]{1,0:T(8,128)(2,1)S(1)}, u32[]{:S(2)}, u32[]{:S(2)}) collective-permute-start(bf16[128,512]{1,0:T(8,128)(2,1)S(1)} %collective-permute-done.9.refs_4_), channel_id=1, source_target_pairs={{0,4},{1,5},{2,6},{3,7},{4,12},{5,13},{6,14},{7,15},{8,0},{9,1},{1... | collective-permute-start | bytes 393224 | tf_op jit(solution)/shard_map/ppermute | solution.py:30
  36.0 0.0 collective-permute-done.8.refs_3_
  36.0 1.6 %collective-permute-start.12 = (bf16[128,512]{1,0:T(8,128)(2,1)S(1)}, bf16[128,512]{1,0:T(8,128)(2,1)S(1)}, u32[]{:S(2)}, u32[]{:S(2)}) collective-permute-start(bf16[128,512]{1,0:T(8,128)(2,1)S(1)} %broadcast_select_fusion), channel_id=1, source_target_pairs={{0,16},{1,13},{2,18},{3,15},{4,8},{5,21},{6,10},{7,23},{8,24},{9,5... | collective-permute-start | bytes 393224 | tf_op jit(solution)/shard_map/ppermute | solution.py:30
  37.6 1.6 %collective-permute-start.10 = (bf16[128,512]{1,0:T(8,128)(2,1)S(1)}, bf16[128,512]{1,0:T(8,128)(2,1)S(1)}, u32[]{:S(2)}, u32[]{:S(2)}) collective-permute-start(bf16[128,512]{1,0:T(8,128)(2,1)S(1)} %collective-permute-done.8.refs_3_), channel_id=1, source_target_pairs={{0,8},{1,9},{2,10},{3,11},{4,0},{5,1},{6,2},{7,3},{8,16},{9,17},{1... | collective-permute-start | bytes 393224 | tf_op jit(solution)/shard_map/ppermute | solution.py:30
  39.2 0.7 %fusion.11.where_ref = s32[17]{0:T(128)S(1)} fusion(s32[32,17]{1,0:T(8,128)} %constant.55.clone, s32[]{:T(128)S(6)} %select_n.60), kind=kLoop, calls=%fused_computation.27 | loop fusion | bytes 140 | tf_op jit(solution)/shard_map/squeeze | solution.py:138
  39.9 1.5 %collective-permute-done.11.refs_6_ = bf16[128,512]{1,0:T(8,128)(2,1)S(1)} collective-permute-done((bf16[128,512]{1,0:T(8,128)(2,1)S(1)}, bf16[128,512]{1,0:T(8,128)(2,1)S(1)}, u32[]{:S(2)}, u32[]{:S(2)}) %collective-permute-start.11) | collective-permute-done | bytes 131104 | tf_op jit(solution)/shard_map/ppermute | solution.py:30
  41.4 1.7 %collective-permute-done.12.refs_7_ = bf16[128,512]{1,0:T(8,128)(2,1)S(1)} collective-permute-done((bf16[128,512]{1,0:T(8,128)(2,1)S(1)}, bf16[128,512]{1,0:T(8,128)(2,1)S(1)}, u32[]{:S(2)}, u32[]{:S(2)}) %collective-permute-start.12) | collective-permute-done | bytes 131104 | tf_op jit(solution)/shard_map/ppermute | solution.py:30
  43.1 0.2 collective-permute-done.10.refs_5_
  43.4 1.1 %pair_sums.1 = (f32[256,128]{1,0:T(8,128)S(1)}, bf16[256,128]{1,0:T(8,128)(2,1)S(1)}, bf16[256,128]{1,0:T(8,128)(2,1)S(1)}, bf16[256,128]{1,0:T(8,128)(2,1)S(1)}) custom-call(s32[17]{0:T(128)S(1)} %fusion.11.where_ref, bf16[128,512]{1,0:T(8,128)(2,1)S(1)} %fusion.refs_0_, bf16[128,512]{1,0:T(8,128)(2,1)S(1)} %collective-permute-done.6.refs_1_, ...), custom_call_target="tpu_custom_call" | custom-call | tf_op jit(solution)/shard_map/pair_sums/pallas_call | solution.py:141
  44.4 0.1 collective-permute-start.13
  44.5 1.6 %collective-permute-start.14 = (bf16[256,128]{1,0:T(8,128)(2,1)S(1)}, bf16[256,128]{1,0:T(8,128)(2,1)S(1)}, u32[]{:S(2)}, u32[]{:S(2)}) collective-permute-start(bf16[256,128]{1,0:T(8,128)(2,1)S(1)} %get-tuple-element.15), channel_id=1, source_target_pairs={{0,2},{1,3},{2,0},{3,1},{4,6},{5,7},{6,4},{7,5},{8,10},{9,11},{10,... | collective-permute-start | bytes 196616 | tf_op jit(solution)/shard_map/ppermute | solution.py:30
  46.1 0.3 collective-permute-start.15
  46.4 0.0 collective-permute-done.13
  46.4 2.6 %collective-permute-done.14 = bf16[256,128]{1,0:T(8,128)(2,1)S(1)} collective-permute-done((bf16[256,128]{1,0:T(8,128)(2,1)S(1)}, bf16[256,128]{1,0:T(8,128)(2,1)S(1)}, u32[]{:S(2)}, u32[]{:S(2)}) %collective-permute-start.14) | collective-permute-done | bytes 65568 | tf_op jit(solution)/shard_map/ppermute | solution.py:30
  49.0 1.1 %collective-permute-done.15 = bf16[256,128]{1,0:T(8,128)(2,1)S(1)} collective-permute-done((bf16[256,128]{1,0:T(8,128)(2,1)S(1)}, bf16[256,128]{1,0:T(8,128)(2,1)S(1)}, u32[]{:S(2)}, u32[]{:S(2)}) %collective-permute-start.15) | collective-permute-done | bytes 65568 | tf_op jit(solution)/shard_map/ppermute | solution.py:30
  50.1 0.7 %add_multiply_fusion = f32[256,128]{1,0:T(8,128)} fusion(bf16[256,128]{1,0:T(8,128)(2,1)S(1)} %collective-permute-done.15, bf16[256,128]{1,0:T(8,128)(2,1)S(1)} %collective-permute-done.14, f32[256,128]{1,0:T(8,128)S(1)} %get-tuple-element.13, bf16[256,128]{1,0:T(8,128)(2,1)S(1)} %collective-permute-done.13), kind=kLoop, calls=%fused_computation.16 | loop fusion | flops 229376 | bytes 458752 | tf_op jit(solution)/shard_map/div | solution.py:153
  (8 shorter events, 0.1 us)
Async XLA Ops:
  0.0 1.7 %copy-start = (bf16[512,1024]{1,0:T(8,128)(2,1)S(1)}, bf16[512,1024]{1,0:T(8,128)(2,1)}, u32[]{:S(2)}) copy-start(bf16[512,1024]{1,0:T(8,128)(2,1)} %param.5) | copy-start | bytes 3145732
  1.0 2.8 %collective-permute-start.1 = (bf16[512,128]{1,0:T(8,128)(2,1)S(1)}, bf16[512,128]{1,0:T(8,128)(2,1)S(1)}, u32[]{:S(2)}, u32[]{:S(2)}) collective-permute-start(bf16[512,128]{1,0:T(8,128)(2,1)S(1)} %dynamic-slice_bitcast_fusion), channel_id=1, source_target_pairs={{0,0},{1,1},{2,2},{3,3},{4,8},{5,9},{6,10},{7,11},{8,4},{9,5},{10,... | collective-permute-start | bytes 393224 | tf_op jit(solution)/shard_map/ppermute | solution.py:30
  3.2 0.7 %copy-start.1 = (s32[128]{0:T(128)S(1)}, s32[128]{0:T(128)}, u32[]{:S(2)}) copy-start(s32[128]{0:T(128)} %param.8) | copy-start | bytes 1540
  3.2 0.7 %copy-start.2 = (s32[128]{0:T(128)S(1)}, s32[128]{0:T(128)}, u32[]{:S(2)}) copy-start(s32[128]{0:T(128)} %param.7) | copy-start | bytes 1540
  3.8 9.3 %collective-permute-start.2 = (bf16[512,128]{1,0:T(8,128)(2,1)S(1)}, bf16[512,128]{1,0:T(8,128)(2,1)S(1)}, u32[]{:S(2)}, u32[]{:S(2)}) collective-permute-start(bf16[512,128]{1,0:T(8,128)(2,1)S(1)} %collective-permute-done.1), channel_id=1, source_target_pairs={{0,1},{1,0},{2,3},{3,2},{4,5},{5,4},{6,7},{7,6},{8,9},{9,8},{10,11... | collective-permute-start | bytes 393224 | tf_op jit(solution)/shard_map/ppermute | solution.py:30
  5.4 12.1 %collective-permute-start = (bf16[528,128]{1,0:T(8,128)(2,1)S(1)}, bf16[528,128]{1,0:T(8,128)(2,1)S(1)}, u32[]{:S(2)}, u32[]{:S(2)}) collective-permute-start(bf16[528,128]{1,0:T(8,128)(2,1)S(1)} %pad_maximum_fusion), channel_id=1, source_target_pairs={{0,4},{1,5},{2,6},{3,7},{4,0},{5,1},{6,2},{7,3},{8,12},{9,13},{10,... | collective-permute-start | bytes 405512 | tf_op jit(solution)/shard_map/ppermute | solution.py:30
  13.1 7.1 %collective-permute-start.4 = (f16[128,512]{1,0:T(8,128)(2,1)S(1)}, f16[128,512]{1,0:T(8,128)(2,1)S(1)}, u32[]{:S(2)}, u32[]{:S(2)}) collective-permute-start(f16[128,512]{1,0:T(8,128)(2,1)S(1)} %multiply_convert_fusion.1), channel_id=1, source_target_pairs={{0,4},{1,5},{2,6},{3,7},{4,0},{5,1},{6,2},{7,3},{8,12},{9,13},{10,... | collective-permute-start | bytes 393224 | tf_op jit(solution)/shard_map/ppermute | solution.py:30
  17.5 2.2 %collective-permute-start.3 = (bf16[512,128]{1,0:T(8,128)(2,1)S(1)}, bf16[512,128]{1,0:T(8,128)(2,1)S(1)}, u32[]{:S(2)}, u32[]{:S(2)}) collective-permute-start(bf16[512,128]{1,0:T(8,128)(2,1)S(1)} %slice.10), channel_id=1, source_target_pairs={{0,1},{1,0},{2,3},{3,2},{4,5},{5,4},{6,7},{7,6},{8,9},{9,8},{10,11... | collective-permute-start | bytes 393224 | tf_op jit(solution)/shard_map/ppermute | solution.py:30
  17.6 6.2 %collective-permute-start.5 = (f16[128,512]{1,0:T(8,128)(2,1)S(1)}, f16[128,512]{1,0:T(8,128)(2,1)S(1)}, u32[]{:S(2)}, u32[]{:S(2)}) collective-permute-start(f16[128,512]{1,0:T(8,128)(2,1)S(1)} %multiply_convert_fusion), channel_id=1, source_target_pairs={{0,4},{1,5},{2,6},{3,7},{4,12},{5,13},{6,14},{7,15},{8,0},{9,1},{1... | collective-permute-start | bytes 393224 | tf_op jit(solution)/shard_map/ppermute | solution.py:30
  24.3 5.3 %collective-permute-start.7 = (bf16[128,512]{1,0:T(8,128)(2,1)S(1)}, bf16[128,512]{1,0:T(8,128)(2,1)S(1)}, u32[]{:S(2)}, u32[]{:S(2)}) collective-permute-start(bf16[128,512]{1,0:T(8,128)(2,1)S(1)} %fusion.refs_0_), channel_id=1, source_target_pairs={{0,4},{1,5},{2,6},{3,7},{4,12},{5,13},{6,14},{7,15},{8,0},{9,1},{1... | collective-permute-start | bytes 393224 | tf_op jit(solution)/shard_map/ppermute | solution.py:30
  26.1 5.0 %collective-permute-start.6 = (bf16[128,512]{1,0:T(8,128)(2,1)S(1)}, bf16[128,512]{1,0:T(8,128)(2,1)S(1)}, u32[]{:S(2)}, u32[]{:S(2)}) collective-permute-start(bf16[128,512]{1,0:T(8,128)(2,1)S(1)} %fusion.refs_0_), channel_id=1, source_target_pairs={{0,8},{1,9},{2,10},{3,11},{4,0},{5,1},{6,2},{7,3},{8,16},{9,17},{1... | collective-permute-start | bytes 393224 | tf_op jit(solution)/shard_map/ppermute | solution.py:30
  29.6 5.0 %collective-permute-start.9 = (bf16[128,512]{1,0:T(8,128)(2,1)S(1)}, bf16[128,512]{1,0:T(8,128)(2,1)S(1)}, u32[]{:S(2)}, u32[]{:S(2)}) collective-permute-start(bf16[128,512]{1,0:T(8,128)(2,1)S(1)} %collective-permute-done.7.refs_2_), channel_id=1, source_target_pairs={{0,4},{1,5},{2,6},{3,7},{4,12},{5,13},{6,14},{7,15},{8,0},{9,1},{1... | collective-permute-start | bytes 393224 | tf_op jit(solution)/shard_map/ppermute | solution.py:30
  31.1 5.0 %collective-permute-start.8 = (bf16[128,512]{1,0:T(8,128)(2,1)S(1)}, bf16[128,512]{1,0:T(8,128)(2,1)S(1)}, u32[]{:S(2)}, u32[]{:S(2)}) collective-permute-start(bf16[128,512]{1,0:T(8,128)(2,1)S(1)} %collective-permute-done.6.refs_1_), channel_id=1, source_target_pairs={{0,8},{1,9},{2,10},{3,11},{4,0},{5,1},{6,2},{7,3},{8,16},{9,17},{1... | collective-permute-start | bytes 393224 | tf_op jit(solution)/shard_map/ppermute | solution.py:30
  34.6 6.8 %collective-permute-start.11 = (bf16[128,512]{1,0:T(8,128)(2,1)S(1)}, bf16[128,512]{1,0:T(8,128)(2,1)S(1)}, u32[]{:S(2)}, u32[]{:S(2)}) collective-permute-start(bf16[128,512]{1,0:T(8,128)(2,1)S(1)} %collective-permute-done.9.refs_4_), channel_id=1, source_target_pairs={{0,4},{1,5},{2,6},{3,7},{4,12},{5,13},{6,14},{7,15},{8,0},{9,1},{1... | collective-permute-start | bytes 393224 | tf_op jit(solution)/shard_map/ppermute | solution.py:30
  36.0 7.1 %collective-permute-start.12 = (bf16[128,512]{1,0:T(8,128)(2,1)S(1)}, bf16[128,512]{1,0:T(8,128)(2,1)S(1)}, u32[]{:S(2)}, u32[]{:S(2)}) collective-permute-start(bf16[128,512]{1,0:T(8,128)(2,1)S(1)} %broadcast_select_fusion), channel_id=1, source_target_pairs={{0,16},{1,13},{2,18},{3,15},{4,8},{5,21},{6,10},{7,23},{8,24},{9,5... | collective-permute-start | bytes 393224 | tf_op jit(solution)/shard_map/ppermute | solution.py:30
  37.6 5.8 %collective-permute-start.10 = (bf16[128,512]{1,0:T(8,128)(2,1)S(1)}, bf16[128,512]{1,0:T(8,128)(2,1)S(1)}, u32[]{:S(2)}, u32[]{:S(2)}) collective-permute-start(bf16[128,512]{1,0:T(8,128)(2,1)S(1)} %collective-permute-done.8.refs_3_), channel_id=1, source_target_pairs={{0,8},{1,9},{2,10},{3,11},{4,0},{5,1},{6,2},{7,3},{8,16},{9,17},{1... | collective-permute-start | bytes 393224 | tf_op jit(solution)/shard_map/ppermute | solution.py:30
  44.4 1.9 %collective-permute-start.13 = (bf16[256,128]{1,0:T(8,128)(2,1)S(1)}, bf16[256,128]{1,0:T(8,128)(2,1)S(1)}, u32[]{:S(2)}, u32[]{:S(2)}) collective-permute-start(bf16[256,128]{1,0:T(8,128)(2,1)S(1)} %get-tuple-element.14), channel_id=1, source_target_pairs={{0,1},{1,0},{2,3},{3,2},{4,5},{5,4},{6,7},{7,6},{8,9},{9,8},{10,11... | collective-permute-start | bytes 196616 | tf_op jit(solution)/shard_map/ppermute | solution.py:30
  44.5 4.5 %collective-permute-start.14 = (bf16[256,128]{1,0:T(8,128)(2,1)S(1)}, bf16[256,128]{1,0:T(8,128)(2,1)S(1)}, u32[]{:S(2)}, u32[]{:S(2)}) collective-permute-start(bf16[256,128]{1,0:T(8,128)(2,1)S(1)} %get-tuple-element.15), channel_id=1, source_target_pairs={{0,2},{1,3},{2,0},{3,1},{4,6},{5,7},{6,4},{7,5},{8,10},{9,11},{10,... | collective-permute-start | bytes 196616 | tf_op jit(solution)/shard_map/ppermute | solution.py:30
  46.1 4.1 %collective-permute-start.15 = (bf16[256,128]{1,0:T(8,128)(2,1)S(1)}, bf16[256,128]{1,0:T(8,128)(2,1)S(1)}, u32[]{:S(2)}, u32[]{:S(2)}) collective-permute-start(bf16[256,128]{1,0:T(8,128)(2,1)S(1)} %get-tuple-element.16), channel_id=1, source_target_pairs={{0,3},{1,2},{2,1},{3,0},{4,7},{5,6},{6,5},{7,4},{8,11},{9,10},{10,... | collective-permute-start | bytes 196616 | tf_op jit(solution)/shard_map/ppermute | solution.py:30
